TPU v7x, 32 devices: a whole 2x2x4 slice. The times are simulated.
32 devices in a mesh: ctx: 8 (over y, x, core), fsdp: 4 (over z).
Axes of the slice: x: 2, y: 2, z: 4, core: 2. Of those that a mesh axis runs over, the one named last changes fastest.
Arguments:
- hidden_in: bfloat16 [4, 1024, 1024], P('fsdp', 'ctx'), may hold values from -6 to 6
- encoder_out: bfloat16 [4, 2048, 1024], P('fsdp', 'ctx'), may hold values from -6 to 6
- doc_ids: int32 [4, 1024], P('fsdp'), may hold values from 0 to 3, as said below
- enc_offsets: int32 [4, 4], P('fsdp'), may hold values from 0 to 1536, as said below
- cotangent: bfloat16 [4, 1024, 1024], P('fsdp', 'ctx'), may hold values from -6 to 6
- self_qkv: bfloat16 [1024, 3072], P('fsdp'), may hold values from -0.09375 to 0.09375
- self_out: bfloat16 [1024, 1024], P('fsdp'), may hold values from -0.75 to 0.75
- rel_bias: bfloat16 [32, 16], P('fsdp'), may hold values from -4 to 4
- cross_q: bfloat16 [1024, 1024], P('fsdp'), may hold values from -0.09375 to 0.09375
- cross_kv: bfloat16 [1024, 2048], P('fsdp'), may hold values from -0.09375 to 0.09375
- cross_out: bfloat16 [1024, 1024], P('fsdp'), may hold values from -0.75 to 0.75
- ffn_in: bfloat16 [1024, 5632], P('fsdp'), may hold values from -0.1875 to 0.1875
- ffn_out: bfloat16 [2816, 1024], P('fsdp'), may hold values from -0.109375 to 0.109375
- norm_gains: bfloat16 [3, 1024], P(None, 'fsdp'), may hold values from 0.5 to 1.5
Outputs:
- output: bfloat16 [4, 1024, 1024], P('fsdp', 'ctx')
- grad_hidden: float32 [4, 1024, 1024], P('fsdp', 'ctx')
- grad_encoder: float32 [4, 2048, 1024], P('fsdp', 'ctx')
- grad_self_qkv: float32 [1024, 3072], P('fsdp')
- grad_self_out: float32 [1024, 1024], P('fsdp')
- grad_rel_bias: float32 [32, 16], P('fsdp')
- grad_cross_q: float32 [1024, 1024], P('fsdp')
- grad_cross_kv: float32 [1024, 2048], P('fsdp')
- grad_cross_out: float32 [1024, 1024], P('fsdp')
- grad_ffn_in: float32 [1024, 5632], P('fsdp')
- grad_ffn_out: float32 [2816, 1024], P('fsdp')
- grad_norm_gains: float32 [3, 1024], P(None, 'fsdp')
Inputs may be any that keep to these rules, and one draw needn't show every extreme that they name: In each stream doc_ids never falls along positions; each of the 4 documents has 1 to 682 tokens, and one has exactly 682. In each stream the offsets are distinct multiples of 512; document d attends encoder rows enc_offsets[d] to enc_offsets[d] + 511 of its stream.
All inputs are finite; a program needn't handle non-finite values.
Results may differ from a plain program's by a relative error of at most 0.034.
The roundings to bfloat16 on the way count: a program that leaves them out, or rounds other values in their place, can miss the bound.
Values may be sent and summed in bfloat16 or wider, within the bound.
No kernel may reach another device: no remote copies, remote signals or barrier semaphores. Data moves between devices by JAX's collectives and lax.ppermute only.
A program may use at most 320 MiB of HBM per device.

v0:
```python
import functools
import math

import jax
import jax.numpy as jnp
import numpy as np
from jax import lax
from jax.experimental import pallas as pl
from jax.experimental.pallas import tpu as pltpu
from jax.sharding import PartitionSpec as P

D = 1024
H = 16
DK = 64
FF = 2816
BUCKETS = 32
ENC_ROWS = 512
QB = 128
NEG = -1e30
EPSILON = 1e-06
BF = jnp.bfloat16
F32 = jnp.float32

EDGES = np.ceil(16.0 * 8.0 ** (np.arange(1, 16) / 16.0)).astype(np.int32)


def near_buckets():
    gap = np.arange(-3, 4)[:, None, None] * 64 + (np.arange(QB) // 64 * 128 + np.arange(QB) % 64)[None, None, :]
    steps = np.maximum(gap - np.arange(64)[None, :, None], 0)
    far = 16 + np.sum(steps[..., None] >= EDGES, axis=-1)
    return np.where(steps < 16, steps, far).astype(np.int32)


def dot(a, b):
    return jnp.dot(a, b, preferred_element_type=F32)


def dot_nt(a, b):
    return lax.dot_general(a, b, (((1,), (1,)), ((), ())), preferred_element_type=F32)


def dot_tn(a, b):
    return lax.dot_general(a, b, (((0,), (0,)), ((), ())), preferred_element_type=F32)


def send(value, axis, count, target):
    return lax.ppermute(value, axis, [(i, target(i)) for i in range(count)])


def first_way(i):
    return i ^ 2 if i % 2 == 0 else i ^ 4


def second_way(i):
    return i ^ 4 if i % 2 == 0 else i ^ 2


def ctx_order(me, count):
    if count == 8:
        even = (me % 2) == 0
        one, two = jnp.where(even, 2, 4), jnp.where(even, 4, 2)
        rel = [0, one, two, 6, 1, jnp.where(even, 5, 3), jnp.where(even, 3, 5), 7]
    else:
        rel = list(range(count))
    return [me ^ r for r in rel]


def ctx_gather(value, count):
    if count == 8:
        near, other = send(value, "ctx", 8, first_way), send(value, "ctx", 8, second_way)
        far = send(near, "ctx", 8, second_way)
        mine = [value, near, other, far]
        return mine + [send(v, "ctx", 8, lambda i: i ^ 1) for v in mine]
    return [value] + [send(value, "ctx", count, lambda i, d=d: i ^ d) for d in range(1, count)]


def chip_order(me, count):
    return [(me // 2) ^ r for r in range(count // 2)]


def chip_gather(value, count):
    return [value] + [send(value, "ctx", count, lambda i, d=d: i ^ (2 * d)) for d in range(1, count // 2)]


def chip_reduce(away, count):
    return [send(away[d - 1], "ctx", count, lambda i, d=d: i ^ (2 * d)) for d in range(1, count // 2)]


def sibling(value, count):
    return send(value, "ctx", count, lambda i: i ^ 1)


def after(value, *others):
    return lax.optimization_barrier((value, *others))[0]


def z_gather(value, depth):
    return [value] + [send(value, "fsdp", depth, lambda i, d=d: i ^ d) for d in range(1, depth)]


def stack_heads(rows, heads):
    if heads == 1:
        return rows
    lane = lax.broadcasted_iota(jnp.int32, rows.shape, 1) // DK
    return jnp.concatenate([jnp.where(lane == h, rows, jnp.zeros_like(rows)) for h in range(heads)], axis=0)


def unstack_heads(cols, heads):
    parts = [cols[h * DK : (h + 1) * DK, h * QB : (h + 1) * QB] for h in range(heads)]
    return jnp.concatenate(parts, axis=0).T if heads > 1 else parts[0].T


def tile_lanes(row, heads):
    return jnp.concatenate([row] * heads, axis=1) if heads > 1 else row


def block_place(l, core, chips):
    return 2 * l + (core if l < chips else 1 - core)


def self_scores(q_ref, k_ref, near_ref, start_ref, place_ref, block, shift, heads):
    rows = pl.ds(block * QB, QB)
    stacked = stack_heads(q_ref[rows, :], heads)
    starts = tile_lanes(start_ref[:, rows], heads)
    places = tile_lanes(place_ref[:, rows], heads)
    tiles = []
    for kb in range(2 * block + 2):
        score = dot_nt(k_ref[pl.ds(kb * QB, QB), :], stacked)
        if kb >= 2 * block - 1:
            first = 4 * block - 2 * kb + shift + 3
            score = score + jnp.concatenate([near_ref[first], near_ref[first - 1]], axis=0)
        at = lax.broadcasted_iota(jnp.int32, score.shape, 0) + kb * QB
        keep = at >= starts
        if kb >= 2 * block:
            keep = keep & (at <= places)
        tiles.append(jnp.where(keep, score, NEG))
    return stacked, tiles


def fold(op, tiles, reduce):
    return functools.reduce(op, [reduce(t, axis=0, keepdims=True) for t in tiles])


def self_forward(heads, core, q_ref, k_ref, v_ref, near_ref, start_ref, place_ref, o_ref, lse_ref, vt_ref):
    blocks = q_ref.shape[0] // QB
    vt_ref[...] = v_ref[...].T
    for block in range(blocks):
        shift = core if block < blocks // 2 else 1 - core
        _, tiles = self_scores(q_ref, k_ref, near_ref, start_ref, place_ref, block, shift, heads)
        top = fold(jnp.maximum, tiles, jnp.max)
        tiles = [jnp.exp(t - top) for t in tiles]
        total = fold(jnp.add, tiles, jnp.sum)
        inverse = 1.0 / total
        probs = jnp.concatenate([(t * inverse).astype(BF) for t in tiles], axis=0)
        out = dot(vt_ref[:, pl.ds(0, (block + 1) * 2 * QB)], probs)
        o_ref[pl.ds(block * QB, QB), :] = unstack_heads(out, heads).astype(BF)
        lse_ref[:, pl.ds(block * QB * heads, QB * heads)] = top + jnp.log(total)


def self_backward(heads, core, q_ref, k_ref, v_ref, do_ref, lse_ref, near_ref, start_ref, place_ref, dq_ref, dkv_ref, dnear_ref, dfar_ref, ds_ref, p_ref, kt_ref):
    blocks = q_ref.shape[0] // QB
    width = q_ref.shape[1]
    wide = heads * QB

    def spot(kb, block):
        row, first = (kb, 0) if kb < blocks // 2 else (blocks - 1 - kb, kb + 1)
        return row, (first + block - kb) * wide

    kt_ref[...] = k_ref[...].T
    dnear_ref[...] = jnp.zeros_like(dnear_ref)
    far = jnp.zeros((1, wide), F32)
    for block in range(blocks):
        shift = core if block < blocks // 2 else 1 - core
        _, tiles = self_scores(q_ref, k_ref, near_ref, start_ref, place_ref, block, shift, heads)
        douts = stack_heads(do_ref[pl.ds(block * QB, QB), :], heads)
        lse = lse_ref[:, pl.ds(block * wide, wide)]
        probs = [jnp.exp(t - lse) for t in tiles]
        dprobs = [dot_nt(v_ref[pl.ds(kb * QB, QB), :], douts) for kb in range(len(tiles))]
        delta = functools.reduce(jnp.add, [jnp.sum(a * b, axis=0, keepdims=True) for a, b in zip(probs, dprobs)])
        dscores = []
        for kb in range(len(tiles)):
            dscore = (probs[kb] * (dprobs[kb] - delta)).astype(BF)
            row, first = spot(kb // 2, block)
            at = pl.ds(kb % 2 * QB, QB), pl.ds(first, wide)
            ds_ref[row, at[0], at[1]] = dscore
            p_ref[row, at[0], at[1]] = probs[kb].astype(BF)
            dscores.append(dscore)
            exact = dscore.astype(F32)
            if kb >= 2 * block - 1:
                first = 4 * block - 2 * kb + shift + 3
                dnear_ref[first] += exact[: QB // 2]
                dnear_ref[first - 1] += exact[QB // 2 :]
            else:
                far = far + jnp.sum(exact, axis=0, keepdims=True)
        dq = dot(kt_ref[:, pl.ds(0, (block + 1) * 2 * QB)], jnp.concatenate(dscores, axis=0))
        dq_ref[pl.ds(block * QB, QB), :] = unstack_heads(dq, heads).astype(BF)
    dfar_ref[...] = far
    queries = jnp.concatenate([stack_heads(q_ref[pl.ds(b * QB, QB), :], heads) for b in range(blocks)], axis=0)
    douts = jnp.concatenate([stack_heads(do_ref[pl.ds(b * QB, QB), :], heads) for b in range(blocks)], axis=0)
    for kb in range(blocks):
        row, first = spot(kb, kb)
        lanes = pl.ds(first, (blocks - kb) * wide)
        rows = pl.ds(kb * 2 * QB, 2 * QB)
        dkv_ref[rows, pl.ds(0, width)] = dot(ds_ref[row, :, lanes], queries[kb * wide :])
        dkv_ref[rows, pl.ds(width, width)] = dot(p_ref[row, :, lanes], douts[kb * wide :])


def cross_forward(heads, count_ref, blocks_ref, docs_ref, offs_ref, q_ref, k_ref, v_ref, doc_ref, o_ref, lse_ref, vt_ref, acc_ref, norm_ref):
    stream = q_ref.shape[0]
    for part in range(v_ref.shape[0] // ENC_ROWS):
        vt_ref[part] = v_ref[pl.ds(part * ENC_ROWS, ENC_ROWS), :].T
    acc_ref[...] = jnp.zeros_like(acc_ref)
    norm_ref[...] = jnp.zeros_like(norm_ref)

    def step(t, carry):
        block, doc, off = blocks_ref[t], docs_ref[t], offs_ref[t]
        stacked = stack_heads(q_ref[pl.ds(pl.multiple_of(block * QB, QB), QB), :], heads)
        keys = k_ref[pl.ds(pl.multiple_of(off * ENC_ROWS, ENC_ROWS), ENC_ROWS), :]
        score = dot_nt(keys, stacked)
        top = jnp.max(score, axis=0, keepdims=True)
        weights = jnp.exp(score - top)
        total = jnp.sum(weights, axis=0, keepdims=True)
        probs = (weights * (1.0 / total)).astype(BF)
        out = dot(vt_ref[off], probs)
        mine = tile_lanes(doc_ref[block], heads) == doc
        acc_ref[block] = jnp.where(mine, out, acc_ref[block])
        norm_ref[block] = jnp.where(mine, top + jnp.log(total), norm_ref[block])
        return carry

    lax.fori_loop(0, count_ref[0], step, 0)
    for block in range(stream // QB):
        o_ref[pl.ds(block * QB, QB), :] = unstack_heads(acc_ref[block], heads).astype(BF)
    lse_ref[...] = norm_ref[...]


def cross_backward(heads, count_ref, blocks_ref, docs_ref, offs_ref, q_ref, k_ref, v_ref, do_ref, doc_ref, lse_ref, dq_ref, kt_ref, acc_ref, dka_ref, dva_ref):
    stream = q_ref.shape[0]
    for part in range(k_ref.shape[0] // ENC_ROWS):
        kt_ref[part] = k_ref[pl.ds(part * ENC_ROWS, ENC_ROWS), :].T
    acc_ref[...] = jnp.zeros_like(acc_ref)
    dka_ref[...] = jnp.zeros_like(dka_ref)
    dva_ref[...] = jnp.zeros_like(dva_ref)

    def step(t, carry):
        block, doc, off = blocks_ref[t], docs_ref[t], offs_ref[t]
        at = pl.ds(pl.multiple_of(block * QB, QB), QB)
        enc = pl.ds(pl.multiple_of(off * ENC_ROWS, ENC_ROWS), ENC_ROWS)
        stacked, douts = stack_heads(q_ref[at, :], heads), stack_heads(do_ref[at, :], heads)
        mine = tile_lanes(doc_ref[block], heads) == doc
        probs = jnp.where(mine, jnp.exp(dot_nt(k_ref[enc, :], stacked) - lse_ref[block]), 0.0)
        dprobs = dot_nt(v_ref[enc, :], douts)
        delta = jnp.sum(probs * dprobs, axis=0, keepdims=True)
        dscore = (probs * (dprobs - delta)).astype(BF)
        acc_ref[block] += dot(kt_ref[off], dscore)
        dka_ref[enc, :] += dot(dscore, stacked)
        dva_ref[enc, :] += dot(probs.astype(BF), douts)
        return carry

    lax.fori_loop(0, count_ref[0], step, 0)
    for block in range(stream // QB):
        dq_ref[pl.ds(block * QB, QB), :] = unstack_heads(acc_ref[block], heads).astype(BF)


def rows_at(start, size):
    if isinstance(start, int):
        return pl.ds(start, size)
    return pl.ds(pl.multiple_of(start, size), size)


def assemble_cols(dst, refs, order):
    if len(refs) == 1:
        dst[...] = refs[0][...]
        return
    width = refs[0].shape[1]
    for j, ref in enumerate(refs):
        dst[:, rows_at(order[j] * width, width)] = ref[...]


def assemble_weight(dst, refs, order, zorder, first=0):
    if len(refs) == 1 and len(refs[0].shape) == 4:
        count, depth, slab, _ = refs[0].shape
        width = dst.shape[1] // count
        for j in range(count):
            for p in range(depth):
                dst[rows_at(zorder[p] * slab, slab), pl.ds(j * width, width)] = refs[0][j, p, :, pl.ds(first, width)]
        return
    depth, slab, _ = refs[0].shape
    if len(refs) == 1:
        dst[...] = refs[0][0]
        return
    width = dst.shape[1] // len(refs)
    for j, ref in enumerate(refs):
        for p in range(depth):
            dst[rows_at(zorder[p] * slab, slab), rows_at(order[j] * width, width)] = ref[p, :, pl.ds(first, width)]


def assemble_slabs(dst, refs, zorder, first=0, slab=None):
    slab = slab or refs[0].shape[0]
    width = dst.shape[1]
    for p, ref in enumerate(refs):
        dst[rows_at(zorder[p] * slab, slab), :] = ref[pl.ds(0, slab), pl.ds(first, width)]


def token_rows(device, count, half):
    return rows_at(device * half, half), rows_at((2 * count - 1 - device) * half, half)


def inverse_rms(value):
    return lax.rsqrt(jnp.mean(value * value, axis=-1, keepdims=True) + EPSILON)


def norm_backward(grad, value, gain):
    scale = inverse_rms(value)
    normed = value * scale
    dnormed = grad * gain
    dvalue = scale * (dnormed - normed * jnp.mean(dnormed * normed, axis=-1, keepdims=True))
    return dvalue, jnp.sum(grad * normed, axis=0, keepdims=True)


def run(kernel, scalars, arrays, outs, scratch, name, share):
    flops, moved = share * 1.15e9, share * 1e6
    smem = pl.BlockSpec(memory_space=pltpu.SMEM)
    vmem = pl.BlockSpec(memory_space=pltpu.VMEM)
    return pl.pallas_call(
        kernel,
        in_specs=[smem] * len(scalars) + [vmem] * len(arrays),
        out_specs=[vmem] * len(outs),
        out_shape=[jax.ShapeDtypeStruct(shape, kind) for shape, kind in outs],
        scratch_shapes=[pltpu.VMEM(shape, kind) for shape, kind in scratch],
        compiler_params=pltpu.CompilerParams(vmem_limit_bytes=60 << 20),
        cost_estimate=pl.CostEstimate(flops=int(flops), bytes_accessed=int(moved), transcendentals=0),
        name=name,
    )(*scalars, *arrays)


def assemble_chip(dst, mine, theirs, zorder, core, slab, half, first=0):
    for p, ref in enumerate(mine):
        rows = rows_at(zorder[p] * slab, slab)
        if not theirs:
            dst[rows, :] = ref[pl.ds(0, slab), pl.ds(first, dst.shape[1])]
            continue
        for t in range(dst.shape[1] // (2 * half)):
            lanes = pl.ds(first + t * half, half)
            dst[rows, rows_at(2 * t * half + core * half, half)] = ref[pl.ds(0, slab), lanes]
            dst[rows, rows_at(2 * t * half + (1 - core) * half, half)] = theirs[p][pl.ds(0, slab), lanes]


def store_chip_pieces(value_rows, chip, chips, half, own_ref, away_refs):
    for d in range(chips):
        low, high = token_rows(chip ^ d, chips, half)
        rows = jnp.concatenate([value_rows(low), value_rows(high)], axis=0)
        if d:
            away_refs[d - 1][...] = rows.astype(BF)
        else:
            own_ref[...] = rows


def pick_first(places, qkv_ref, o1_ref, o2_ref, bias_ref, gains_ref, out_ref):
    slab, size = qkv_ref.shape
    part = pl.program_id(0)
    out_ref[pl.ds(0, slab), :] = jnp.where(part < 3, qkv_ref[...], jnp.where(part == 3, o1_ref[...], o2_ref[...]))
    out_ref[pl.ds(slab, 16), :] = jnp.zeros((16, size), BF)
    for t in range(-(-gains_ref.shape[1] // size)):
        @pl.when(part == t)
        def _():
            out_ref[pl.ds(slab + 8, 3), :] = gains_ref[:, pl.ds(t * size, size)]

    @pl.when(part == 0)
    def _():
        out_ref[pl.ds(slab, bias_ref.shape[0]), pl.ds(0, H)] = bias_ref[...]


def first_weights(at, self_qkv, self_out, cross_out, rel_bias, norm_gains, size):
    slab = self_qkv.shape[0]
    step = H * DK // size
    whole = lambda p, at: (0, 0)
    return pl.pallas_call(
        pick_first,
        grid_spec=pltpu.PrefetchScalarGridSpec(
            num_scalar_prefetch=1,
            grid=(5,),
            in_specs=[
                pl.BlockSpec((slab, size), lambda p, at: (0, jnp.minimum(p, 2) * step + at[0])),
                pl.BlockSpec((slab, size), lambda p, at: (0, at[0])),
                pl.BlockSpec((slab, size), lambda p, at: (0, at[0])),
                pl.BlockSpec(rel_bias.shape, whole),
                pl.BlockSpec(norm_gains.shape, whole),
            ],
            out_specs=pl.BlockSpec((slab + 16, size), lambda p, at: (0, p)),
        ),
        out_shape=jax.ShapeDtypeStruct((slab + 16, 5 * size), BF),
        compiler_params=pltpu.CompilerParams(vmem_limit_bytes=16 << 20),
        cost_estimate=pl.CostEstimate(flops=10**9, bytes_accessed=10**6, transcendentals=0),
        name="first_weights",
    )(at.astype(jnp.int32)[None], self_qkv, self_out, cross_out, rel_bias, norm_gains)


def self_project(chips, depth, sides, heads, place, corder, zorder, ids_ref, *refs):
    hidden, mine, theirs = refs[:chips], refs[chips : chips + depth], refs[chips + depth : chips + depth * sides]
    x_ref, h_ref, q_ref, kv_ref, near_ref, gains_ref, w_ref = refs[chips + depth * sides :]
    half = hidden[0].shape[0] // 2
    slab = D // depth
    width = heads * DK
    aux = [w[pl.ds(slab, 16), :].astype(F32) for w in mine]
    for p in range(depth):
        gains_ref[:, rows_at(zorder[p] * slab, slab)] = aux[p][8:, :slab]
    assemble_chip(w_ref, mine, theirs, zorder, place[0], slab, width // 2)
    per = BUCKETS // depth
    lane = lax.broadcasted_iota(jnp.int32, (per, H), 1)
    for h in range(heads):
        pick = lane == place[1] * heads + h
        bias = [jnp.sum(jnp.where(pick, aux[p][:per, :H], 0.0), axis=1, keepdims=True) for p in range(depth)]
        far = sum(jnp.where(zorder[p] == depth - 1, bias[p][per - 1 : per], 0.0) for p in range(depth))
        for a in range(7):
            tile = jnp.zeros((QB // 2, QB), F32)
            if a not in (0, 6):
                for p in range(depth):
                    for r in range(per):
                        tile = jnp.where(ids_ref[a] == zorder[p] * per + r, bias[p][r : r + 1] - far, tile)
            near_ref[a, :, pl.ds(h * QB, QB)] = tile
    gain = gains_ref[0:1, :]
    for p in range(chips):
        rows = hidden[p][...]
        value = rows.astype(F32)
        low = (value * inverse_rms(value) * gain).astype(BF)
        for part, at in enumerate(token_rows(corder[p], chips, half)):
            x_ref[at, :] = rows[part * half : (part + 1) * half]
            h_ref[at, :] = low[part * half : (part + 1) * half]
    for r in range(0, x_ref.shape[0], 256):
        at = pl.ds(r, 256)
        proj = dot(h_ref[at, :], w_ref[...]).astype(BF)
        q_ref[at, :] = proj[:, :width]
        kv_ref[at, :] = proj[:, width:]


def self_attend(chips, heads, place, q_ref, mine_ref, theirs_ref, near_ref, start_ref, place_ref, k_ref, v_ref, o_ref, lse_ref, vt_ref):
    width = heads * DK
    core = place[0]
    for l in range(2 * chips):
        rows = pl.ds(l * 64, 64)
        for ref, side in ((mine_ref, core), (theirs_ref, 1 - core)):
            at = rows_at(block_place(l, side, chips) * 64, 64)
            k_ref[at, :] = ref[rows, pl.ds(0, width)]
            v_ref[at, :] = ref[rows, pl.ds(width, width)]
    self_forward(heads, core, q_ref, k_ref, v_ref, near_ref, start_ref, place_ref, o_ref, lse_ref, vt_ref)


def slabs(refs, depth, wide, zorder):
    if wide:
        return [refs[0].at[p] for p in range(depth)], [refs[1].at[p] for p in range(depth)], zorder, refs[2:]
    return refs[:depth], [], zorder, refs[depth:]


def encoder_block(chips, depth, wide, place, zorder, enc_ref, *refs):
    mine, theirs, zorder, (kv_ref, w_ref) = slabs(refs, depth, wide, zorder)
    width = kv_ref.shape[1] // 2
    rows = enc_ref.shape[1]
    slab = D // depth
    assemble_chip(w_ref, mine, theirs, zorder, place[0], slab, width // 2, width // 2 if wide else width)
    for j in range(chips):
        kv_ref[pl.ds(j * rows, rows), :] = dot(enc_ref[2 * j + place[0]], w_ref[...]).astype(BF)


def encoder_grad(chips, place, keep_ref, come_ref, w_ref, enc_ref, grad_ref, own_ref, *refs):
    away_refs, (dkv_ref,) = refs[: chips - 1], refs[chips - 1 :]
    rows = keep_ref.shape[0] // chips
    core, chip = place[0], place[1]
    total = jnp.zeros(grad_ref.shape, F32)
    for j in range(chips):
        at = pl.ds(j * rows, rows)
        low = (keep_ref[at, :] + come_ref[at, :].astype(F32)).astype(BF)
        dkv_ref[at, :] = low
        total = total + dot_tn(enc_ref[2 * j + core], low)
    grad_ref[...] = total.astype(BF)
    for d in range(chips):
        part = dot_nt(dkv_ref[rows_at((chip ^ d) * rows, rows), :], w_ref[...])
        if d:
            away_refs[d - 1][...] = part.astype(BF)
        else:
            own_ref[...] = part


def cross_block(n_cols, n_w, depth, wide, heads, chips_rows, place, order, corder, zorder, count_ref, blocks_ref, docs_ref, offs_ref, x_ref, gains_ref, kvm_ref, kvt_ref, doc_ref, *refs):
    pieces, outs = refs[:n_cols], refs[n_cols : n_cols + n_w]
    mine, theirs, slab_order, rest = slabs(refs[n_cols + n_w :], depth, wide, zorder)
    kc_ref, vc_ref, x1_ref, h_ref, q_ref, o_ref, lse_ref, wrows_ref, ob_ref, w_ref, wq_ref, vt_ref, acc_ref, norm_ref = rest
    width = heads * DK
    count = 2 * kvm_ref.shape[0] // chips_rows
    for j in range(count // 2):
        at = pl.ds(j * chips_rows, chips_rows)
        for ref, side in ((kvm_ref, place[0]), (kvt_ref, 1 - place[0])):
            to = rows_at((2 * j + side) * chips_rows, chips_rows)
            kc_ref[to, :] = ref[at, pl.ds(0, width)]
            vc_ref[to, :] = ref[at, pl.ds(width, width)]
    assemble_cols(ob_ref, pieces, corder)
    assemble_weight(w_ref, outs, order, zorder)
    assemble_chip(wq_ref, mine, theirs, slab_order, place[0], D // depth, width // 2)
    wrows_ref[...] = w_ref[rows_at(place[1] * width, width), :]
    gain = gains_ref[1:2, :]
    for r in range(0, x_ref.shape[0], 256):
        at = pl.ds(r, 256)
        x1 = x_ref[at, :].astype(F32) + dot(ob_ref[at, :], w_ref[...])
        x1_ref[at, :] = x1
        low = (x1 * inverse_rms(x1) * gain).astype(BF)
        h_ref[at, :] = low
        q_ref[at, :] = dot(low, wq_ref[...]).astype(BF)
    cross_forward(heads, count_ref, blocks_ref, docs_ref, offs_ref, q_ref, kc_ref, vc_ref, doc_ref, o_ref, lse_ref, vt_ref, acc_ref, norm_ref)


def gelu_parts(gate):
    inner = math.sqrt(2.0 / math.pi)
    square = gate * gate
    slope = jnp.tanh(inner * (gate + 0.044715 * gate * square))
    value = 0.5 * gate * (1.0 + slope)
    grad = 0.5 * (1.0 + slope) + 0.5 * gate * (1.0 - slope * slope) * inner * (1.0 + 3 * 0.044715 * square)
    return value, grad


def unpack_units(packed_ref, in_ref, down_ref, piece):
    depth, _, wide = packed_ref.shape
    slab = D // depth
    third = (packed_ref.shape[1] - slab - piece)
    down_ref[pl.ds(depth * piece, down_ref.shape[0] - depth * piece), :] = jnp.zeros((down_ref.shape[0] - depth * piece, D), BF)
    for z in range(depth):
        in_ref[pl.ds(z * slab, slab), :] = packed_ref[z, pl.ds(0, slab), :]
        down_ref[pl.ds(z * piece, piece), pl.ds(0, wide)] = packed_ref[z, pl.ds(slab, piece), :]
        for t in range(wide // (D - wide)):
            size = min(third, piece - t * third)
            down_ref[pl.ds(z * piece + t * third, size), pl.ds(wide, D - wide)] = packed_ref[z, pl.ds(slab + piece, size), pl.ds(t * (D - wide), D - wide)]


def ffn_block(chips, n_cols, n_w, packed, first, piece, place, order, corder, zorder, x1_ref, gains_ref, *refs):
    grads, refs = refs[:chips], refs[chips:]
    pieces, outs = refs[:n_cols], refs[n_cols : n_cols + n_w]
    units_in = refs[n_cols + n_w : n_cols + n_w + (2 if packed else 4)]
    ocb_ref, g_ref, h_ref, act0_ref, act1_ref, dgu0_ref, dgu1_ref, keep_ref, wrows_ref, down0_ref, down1_ref, own_ref, *rest = refs[n_cols + n_w + len(units_in) :]
    away_refs, (w_ref, in0_ref, in1_ref, x2_ref, dh_ref) = rest[: chips - 1], rest[chips - 1 :]
    half = own_ref.shape[0] // 2
    units = act0_ref.shape[1]
    width = wrows_ref.shape[0]
    if packed:
        unpack_units(units_in[0], in0_ref, down0_ref, piece)
        unpack_units(units_in[1], in1_ref, down1_ref, piece)
    else:
        for dst, src in zip((in0_ref, in1_ref, down0_ref, down1_ref), units_in):
            dst[...] = src[...]
    assemble_cols(ocb_ref, pieces, corder)
    assemble_weight(w_ref, outs, order, zorder, first)
    wrows_ref[...] = w_ref[rows_at(place[1] * width, width), :]
    for p in range(chips):
        for part, at in enumerate(token_rows(corder[p], chips, half)):
            g_ref[at, :] = grads[p][pl.ds(part * half, half), :]
    gain = gains_ref[2:3, :]
    for r in range(0, x1_ref.shape[0], 256):
        at = pl.ds(r, 256)
        x2 = x1_ref[at, :] + dot(ocb_ref[at, :], w_ref[...])
        x2_ref[at, :] = x2
        low = (x2 * inverse_rms(x2) * gain).astype(BF)
        h_ref[at, :] = low
        total = None
        for in_ref, down_ref, act_ref, dgu_ref in ((in0_ref, down0_ref, act0_ref, dgu0_ref), (in1_ref, down1_ref, act1_ref, dgu1_ref)):
            both = dot(low, in_ref[...])
            gate, up = both[:, :units], both[:, units:]
            value, slope = gelu_parts(gate)
            act_ref[at, :] = (value * up).astype(BF)
            dact = dot_nt(g_ref[at, :], down_ref[...])
            dgu = jnp.concatenate([dact * up * slope, dact * value], axis=1).astype(BF)
            dgu_ref[at, :] = dgu
            part = dot_nt(dgu, in_ref[...])
            total = part if total is None else total + part
        dh_ref[at, :] = total
    store_chip_pieces(lambda at: dh_ref[at, :], place[1], chips, half, own_ref, away_refs)
    low, high = token_rows(place[1], chips, half)
    keep_ref[pl.ds(0, half), :] = x2_ref[low, :]
    keep_ref[pl.ds(half, half), :] = x2_ref[high, :]


def ffn_output(chips, place, act0_ref, act1_ref, down0_ref, down1_ref, own_ref, *refs):
    away_refs, (out_ref,) = refs[: chips - 1], refs[chips - 1 :]
    for r in range(0, act0_ref.shape[0], 256):
        at = pl.ds(r, 256)
        out_ref[at, :] = dot(act0_ref[at, :], down0_ref[...]) + dot(act1_ref[at, :], down1_ref[...])
    store_chip_pieces(lambda at: out_ref[at, :], place[1], chips, own_ref.shape[0] // 2, own_ref, away_refs)


def norm_grad(index, arrived, *refs):
    own_ref, value_ref, base_ref, gains_ref, out_ref, low_ref, dgain_ref = refs[arrived:]
    total = own_ref[...]
    for ref in refs[:arrived]:
        total = total + ref[pl.ds(0, total.shape[0]), :].astype(F32)
    dvalue, dgain = norm_backward(total, value_ref[...].astype(F32), gains_ref[index : index + 1, :])
    out = base_ref[...].astype(F32) + dvalue
    out_ref[...] = out
    low_ref[...] = out.astype(BF)
    dgain_ref[...] = dgain


def cross_grad(chips, heads, place, corder, count_ref, blocks_ref, docs_ref, offs_ref, wrows_ref, q_ref, k_ref, v_ref, doc_ref, lse_ref, *refs):
    pieces = refs[:chips]
    g_ref, dq_ref, keep_ref, away_ref, do_ref, kt_ref, acc_ref, dka_ref, dva_ref = refs[chips:]
    half = pieces[0].shape[0] // 2
    width = heads * DK
    core = place[0]
    for p in range(chips):
        for part, at in enumerate(token_rows(corder[p], chips, half)):
            g_ref[at, :] = pieces[p][pl.ds(part * half, half), :]
    for r in range(0, g_ref.shape[0], 256):
        at = pl.ds(r, 256)
        do_ref[at, :] = dot_nt(g_ref[at, :], wrows_ref[...]).astype(BF)
    cross_backward(heads, count_ref, blocks_ref, docs_ref, offs_ref, q_ref, k_ref, v_ref, do_ref, doc_ref, lse_ref, dq_ref, kt_ref, acc_ref, dka_ref, dva_ref)
    rows = keep_ref.shape[0] // chips
    for j in range(chips):
        to = pl.ds(j * rows, rows)
        for src, lanes in ((dka_ref, pl.ds(0, width)), (dva_ref, pl.ds(width, width))):
            keep_ref[to, lanes] = src[rows_at((2 * j + core) * rows, rows), :]
            away_ref[to, lanes] = src[rows_at((2 * j + 1 - core) * rows, rows), :].astype(BF)


def table_sums(heads, ids_ref, dnear_ref, dfar_ref, dtable_ref):
    first = lax.broadcasted_iota(jnp.int32, (QB // 2, QB), 1) < QB // 2
    for h in range(heads):
        lanes = pl.ds(h * QB, QB)
        tiles = [dnear_ref[a, :, lanes] for a in range(7)]
        near = [jnp.where(first, tiles[3 + d] + pltpu.roll(tiles[1 + d], QB // 2, 1), 0.0) for d in range(3)]
        far = sum(jnp.sum(jnp.where(first, 0.0, tiles[a]) if a < 6 else tiles[a], axis=0, keepdims=True) for a in (4, 5, 6))
        sums = []
        for bucket in range(BUCKETS):
            parts = [jnp.where(ids_ref[3 + d] == bucket, near[d], 0.0) for d in range(3)]
            sums.append(jnp.sum(parts[0] + parts[1] + parts[2], axis=0, keepdims=True))
        sums[-1] = sums[-1] + far + dfar_ref[:, lanes]
        dtable_ref[h] = jnp.concatenate(sums, axis=0)


def self_grad(chips, n_cols, n_w, heads, first, place, order, corder, zorder, x1_ref, gb2_ref, own_ref, gains_ref, wo_ref, q_ref, k_ref, v_ref, lse_ref, near_ref, start_ref, place_ref, ids_ref, *refs):
    pieces, outs = refs[:n_cols], refs[n_cols : n_cols + n_w]
    gb1_ref, dq_ref, keep_ref, away_ref, dtable_ref, gx1_ref, dgain_ref, dnear_ref, dfar_ref, dqc_ref, w_ref, dx_ref, do_ref, dkv_ref, ds_ref, p_ref, kt_ref = refs[n_cols + n_w :]
    half = own_ref.shape[0] // 2
    core = place[0]
    assemble_cols(dqc_ref, pieces, corder)
    assemble_weight(w_ref, outs, order, zorder, first)
    gain = gains_ref[1:2, :]
    total = jnp.zeros_like(gain)
    for r in range(0, x1_ref.shape[0], 256):
        at = pl.ds(r, 256)
        dh = dot_nt(dqc_ref[at, :], w_ref[...])
        dvalue, dgain = norm_backward(dh, x1_ref[at, :], gain)
        total = total + dgain
        dx_ref[at, :] = dvalue
        low = (gb2_ref[at, :].astype(F32) + dvalue).astype(BF)
        gb1_ref[at, :] = low
        do_ref[at, :] = dot_nt(low, wo_ref[...]).astype(BF)
    dgain_ref[...] = total
    for part, at in enumerate(token_rows(place[1], chips, half)):
        mine = pl.ds(part * half, half)
        gx1_ref[mine, :] = own_ref[mine, :] + dx_ref[at, :]
    self_backward(heads, core, q_ref, k_ref, v_ref, do_ref, lse_ref, near_ref, start_ref, place_ref, dq_ref, dkv_ref, dnear_ref, dfar_ref, ds_ref, p_ref, kt_ref)
    for l in range(2 * chips):
        rows = pl.ds(l * 64, 64)
        keep_ref[rows, :] = dkv_ref[rows_at(block_place(l, core, chips) * 64, 64), :]
        away_ref[rows, :] = dkv_ref[rows_at(block_place(l, 1 - core, chips) * 64, 64), :].astype(BF)
    table_sums(heads, ids_ref, dnear_ref, dfar_ref, dtable_ref)


def self_close(chips, place, x_ref, dq_ref, keep_ref, come_ref, w_ref, *refs):
    more, (dqkv_ref, dgain_ref, own_ref, *refs) = refs[: chips - 1], refs[chips - 1 :]
    away_refs, (dx_ref,) = refs[: chips - 1], refs[chips - 1 :]
    width = dq_ref.shape[1]
    total = jnp.zeros_like(dgain_ref)
    for r in range(0, dq_ref.shape[0], 256):
        at = pl.ds(r, 256)
        dqkv_ref[at, pl.ds(0, width)] = dq_ref[at, :]
        dqkv_ref[at, pl.ds(width, 2 * width)] = (keep_ref[at, :] + come_ref[at, :].astype(F32)).astype(BF)
        part = dot_nt(dqkv_ref[at, :], w_ref[...])
        dx_ref[at, :] = part
        value = x_ref[at, :].astype(F32)
        total = total + jnp.sum(part * (value * inverse_rms(value)), axis=0, keepdims=True)
    dgain_ref[...] = total
    tokens = own_ref.shape[0]
    for ref, piece in zip(away_refs, more):
        ref[pl.ds(tokens, piece.shape[0]), :] = piece[...]
    firsts = [ref.at[pl.ds(0, tokens)] for ref in away_refs]
    store_chip_pieces(lambda at: dx_ref[at, :], place[1], chips, tokens // 2, own_ref, firsts)


def spread_units(depth, piece, parts_ref, out_ref, down_ref):
    n, slab = parts_ref.shape[0], out_ref.shape[0]
    wide = parts_ref.shape[2]
    third = parts_ref.shape[1] - slab - piece
    for j in range(n):
        down_ref[pl.ds(j * piece, piece), pl.ds(0, wide)] = parts_ref[j, pl.ds(slab, piece), :].astype(F32)
        for t in range(wide // (D - wide)):
            size = min(third, piece - t * third)
            part = parts_ref[j, pl.ds(slab + piece, size), pl.ds(t * (D - wide), D - wide)]
            down_ref[pl.ds(j * piece + t * third, size), pl.ds(wide, D - wide)] = part.astype(F32)
    units = -(-piece * depth // 128) * 128
    for r in range(0, slab, 32):
        at = pl.ds(r, 32)
        values = [parts_ref[j, at, :].astype(F32) for j in range(n)]
        cols = [values[j][:, g * units + z * piece : g * units + (z + 1) * piece] for g in range(2) for z in range(depth) for j in range(n)]
        out_ref[at, :] = jnp.concatenate(cols, axis=1)


def spread_stacked(first, groups, parts_ref, *outs):
    n, slab = parts_ref.shape[0], parts_ref.shape[1]
    width = outs[0].shape[1] // (n * groups[0])
    for out, parts in zip(outs, groups):
        for t in range(parts):
            for j in range(n):
                out[:, pl.ds((t * n + j) * width, width)] = parts_ref[j, :, pl.ds(first + t * width, width)].astype(F32)
        first += parts * width


def spread(groups, heads, order, *refs):
    n = len(refs) - len(groups) - 2
    pieces, (*outs, gain_ref, table_ref) = refs[:n], refs[n:]
    slab = outs[0].shape[0]
    width = pieces[0].shape[1] // sum(groups)
    per = table_ref.shape[0]
    lane = lax.broadcasted_iota(jnp.int32, (per, H), 1)
    gain, table = jnp.zeros(gain_ref.shape, F32), jnp.zeros((per, H), F32)
    for j, ref in enumerate(pieces):
        first = 0
        for out, parts in zip(outs, groups):
            for t in range(parts):
                part = ref[pl.ds(0, slab), pl.ds((first + t) * width, width)]
                out[:, rows_at(t * n * width + order[j] * width, width)] = part.astype(F32)
            first += parts
        extra = ref[pl.ds(slab, 16), :].astype(F32)
        gain = gain + extra[8:11, :slab]
        for h in range(heads):
            table = table + jnp.where(lane == (order[j] // 2) * heads + h, extra[:per, h : h + 1], 0.0)
    gain_ref[...] = gain
    table_ref[...] = table


def body(
    hidden_in,
    encoder_out,
    doc_ids,
    enc_offsets,
    cotangent,
    self_qkv,
    self_out,
    rel_bias,
    cross_q,
    cross_kv,
    cross_out,
    ffn_in,
    ffn_out,
    norm_gains,
):
    n, depth = lax.axis_size("ctx"), lax.axis_size("fsdp")
    me, level = lax.axis_index("ctx"), lax.axis_index("fsdp")
    chips = n // 2
    core, chip = me % 2, me // 2
    tokens = hidden_in.shape[1]
    half = tokens // 2
    mine_tokens = tokens * chips
    stream = tokens * n
    width = D // n
    cols = 2 * width
    heads = H // chips
    slab = D // depth
    piece = FF // (depth * n)
    units = -(-piece * depth // 128) * 128
    fill = units - piece * depth
    enc_rows = encoder_out.shape[1]
    rows_all = enc_rows * n
    wide = n == 8
    own, other = me * width, (me ^ 1) * width
    sides = 2 if wide else 1
    order = jnp.stack(ctx_order(me, n)).astype(jnp.int32)
    corder = jnp.stack(chip_order(me, n)).astype(jnp.int32)
    zorder = jnp.stack([level ^ d for d in range(depth)]).astype(jnp.int32)
    place = jnp.stack([core, chip]).astype(jnp.int32)
    per = BUCKETS // depth

    def columns(value, start, size):
        return lax.dynamic_slice_in_dim(value, start, size, 1)

    def part_columns(value, parts, start, size):
        step = value.shape[1] // parts
        return jnp.concatenate([columns(value, p * step + start, size) for p in range(parts)], axis=1)

    def gather_columns(value):
        if wide:
            return chip_gather(value, n)
        groups = [[2 * k + c for k in range(chips)] for c in range(2)]
        return [lax.all_gather(value, "ctx", axis=1, tiled=True, axis_index_groups=groups)]

    def gather_whole(pieces):
        rows = jnp.zeros((D, width), BF)
        for d, value in enumerate(pieces):
            rows = lax.dynamic_update_slice(rows, value, ((level ^ d) * slab, 0))
        return [lax.all_gather(rows, "ctx", axis=1, tiled=True)[None]]

    def cross_weights(start, size):
        return jnp.concatenate([columns(cross_q, start, size), part_columns(cross_kv, 2, start, size)], axis=1)

    def first_of(at, size):
        return first_weights(at, self_qkv, self_out, cross_out, rel_bias, norm_gains, size)

    encoder = lax.all_gather(encoder_out[0], "ctx", axis=0)
    if wide:
        w_first = z_gather(first_of(me, width), depth)
        hidden = chip_gather(after(hidden_in[0], w_first[1]), n)
        w_first2 = [first_of(me ^ 1, width)] + [sibling(v, n) for v in w_first[1:]]
        ready = (*hidden, *w_first, *w_first2)
        w_out = ctx_gather(jnp.stack([v[:slab, 3 * width :] for v in w_first]), n)
        w_cout, first_cout = w_out, width
        w_cross, w_cross2 = None, None
    else:
        w_first, w_first2 = z_gather(first_of(chip, cols), depth), []
        hidden = chip_gather(hidden_in[0], n)
        w_cross, w_cross2 = z_gather(cross_weights(chip * cols, cols), depth), []
        first_cout = 0
        w_out, w_cq, w_cout = [gather_whole(z_gather(columns(w, own, width), depth)) for w in (self_out, cross_q, cross_out)]
    parts = []
    for part in range(2):
        parts += [columns(ffn_in, part * FF + z * (FF // depth) + me * piece, piece) for z in range(depth)]
        parts += [jnp.zeros((slab, fill), BF)] * (fill > 0)
    unit_in = jnp.concatenate(parts, axis=1)
    unit_down = lax.dynamic_slice_in_dim(ffn_out, me * piece, piece)
    if wide:
        third = -(-piece // 24) * 8
        tail = jnp.pad(unit_down[:, 2 * units :], ((0, 3 * third - piece), (0, 0)))
        tail = jnp.concatenate([tail[t * third : (t + 1) * third] for t in range(3)], axis=1)
        packed = jnp.concatenate([unit_in, unit_down[:, : 2 * units], tail], axis=0)
    else:
        w_in = lax.all_gather(unit_in, "fsdp", axis=0, tiled=True)
        w_down = jnp.pad(lax.all_gather(unit_down, "fsdp", axis=0, tiled=True), ((0, fill), (0, 0)))
        w_units = [w_in, sibling(w_in, n), w_down, sibling(w_down, n)]

    ids = doc_ids[0]
    offsets = enc_offsets[0]
    docs = offsets.shape[0]
    doc_range = jnp.arange(docs, dtype=jnp.int32)

    def local_tokens(value):
        low, high = value[: stream // 2].reshape(chips, 2, half), value[stream // 2 :].reshape(chips, 2, half)
        low = jnp.where(core == 0, low[:, 0], low[:, 1])
        high = jnp.where(core == 0, high[:, 1], high[:, 0])
        return jnp.concatenate([low, high], axis=0).reshape(mine_tokens)

    doc_starts = jnp.sum((ids[None, :] < doc_range[:, None]).astype(jnp.int32), axis=1)
    my_ids = local_tokens(ids)
    places = local_tokens(jnp.arange(stream, dtype=jnp.int32))[None]
    starts = jnp.sum(jnp.where(my_ids[None, :] == doc_range[:, None], doc_starts[:, None], 0), axis=0)[None]
    q_blocks = mine_tokens // QB
    first_doc = my_ids[::QB]
    spans = my_ids[QB - 1 :: QB] - first_doc + 1
    at_or_before = np.arange(q_blocks)[:, None] >= np.arange(q_blocks)[None, :]
    ends = jnp.sum(jnp.where(at_or_before, spans[None, :], 0), axis=1)
    slots = jnp.arange(q_blocks + docs, dtype=jnp.int32)
    slot_block = jnp.minimum(jnp.sum((slots[:, None] >= ends[None, :]).astype(jnp.int32), axis=1), q_blocks - 1)
    in_block = slot_block[:, None] == jnp.arange(q_blocks)[None, :]
    slot_doc = slots + jnp.sum(jnp.where(in_block, (first_doc - ends + spans)[None, :], 0), axis=1)
    slot_doc = jnp.clip(slot_doc, 0, docs - 1)
    slot_part = jnp.sum(jnp.where(slot_doc[:, None] == doc_range[None, :], (offsets // ENC_ROWS)[None, :], 0), axis=1)
    work = (jnp.sum(spans)[None], slot_block, slot_doc, slot_part)
    doc_rows = my_ids.reshape(q_blocks, 1, QB)
    near_ids = jnp.asarray(near_buckets())

    rows_bf = ((mine_tokens, cols), BF)
    full_bf = ((mine_tokens, D), BF)
    full_f32 = ((mine_tokens, D), F32)
    own_f32 = ((tokens, D), F32)
    pieces_out = [own_f32] + [((tokens, D), BF)] * (chips - 1)
    lanes = QB * heads
    near_f32 = ((7, QB // 2, lanes), F32)
    triangle = ((q_blocks // 2, 2 * QB, (q_blocks + 1) * lanes), BF)
    parted = ((rows_all // ENC_ROWS, cols, ENC_ROWS), BF)
    blocked = ((q_blocks, cols, lanes), F32)

    x, h1, query, kv, near, gains, wqkv = run(
        functools.partial(self_project, chips, depth, sides, heads), (place, corder, zorder), (near_ids, *hidden, *w_first, *w_first2),
        [full_bf, full_bf, rows_bf, ((mine_tokens, 2 * cols), BF), near_f32, ((8, D), F32), ((D, 3 * cols), BF)],
        [], "self_project", 1)
    if wide:
        w_cross = z_gather(after(cross_weights(own, width), query), depth)
    key, value, attended, lse = run(
        functools.partial(self_attend, chips, heads), (place,), (query, kv, sibling(kv, n), near, starts, places),
        [((stream, cols), BF), ((stream, cols), BF), rows_bf, ((1, mine_tokens * heads), F32)],
        [((cols, stream), BF)], "self_attend", 1)
    ob = gather_columns(attended)
    if wide:
        w_cross = [jnp.stack(list(lax.optimization_barrier((*w_cross, attended))[:depth]))]
        w_cross2 = [sibling(w_cross[0], n)]
    if wide:
        packed = lax.all_gather(after(packed, w_cross[0]), "fsdp", axis=0)
    ckv, wckv = run(
        functools.partial(encoder_block, chips, depth, wide), (place, zorder), (encoder, *w_cross, *w_cross2),
        [((rows_all // 2, 2 * cols), BF), ((D, 2 * cols), BF)], [], "encoder_block", 1)
    ckey, cvalue, x1, h2, cquery, crossed, clse, wo_rows, ob_all = run(
        functools.partial(cross_block, len(ob), len(w_out), depth, wide, heads, enc_rows), (place, order, corder, zorder, *work),
        (x, gains, ckv, sibling(ckv, n), doc_rows, *ob, *w_out, *w_cross, *w_cross2),
        [((rows_all, cols), BF)] * 2 + [full_f32, full_bf, rows_bf, rows_bf, ((q_blocks, 1, lanes), F32), ((cols, D), BF), full_bf],
        [((D, D), BF), ((D, cols), BF), parted, blocked, ((q_blocks, 1, lanes), F32)],
        "cross_block", 6)
    g_pieces = chip_gather(after(cotangent[0], ob[-1]), n)
    ocb_pieces = gather_columns(after(crossed, *g_pieces[1:]))
    if wide:
        w_units = [packed, sibling(after(packed, *ocb_pieces[1:]), n)]
    ocb, g, h3, act, act2, dgu, dgu2, x2_own, wco_rows, down, down2, *dh3 = run(
        functools.partial(ffn_block, chips, len(ocb_pieces), len(w_cout), wide, first_cout, piece), (place, order, corder, zorder),
        (x1, gains, *g_pieces, *ocb_pieces, *w_cout, *w_units),
        [full_bf, full_bf, full_bf, *[((mine_tokens, units), BF)] * 2, *[((mine_tokens, 2 * units), BF)] * 2, own_f32, ((cols, D), BF), *[((units, D), BF)] * 2, *pieces_out],
        [((D, D), BF), *[((D, 2 * units), BF)] * 2, full_f32, full_f32], "ffn_block", 14)

    if wide:
        w_cq = [lax.all_gather(after(w_cross[0][:, :, :width], crossed), "ctx", axis=0)]

    def reduce_norm(parts, index, kept, base):
        arrived = chip_reduce(parts[1:], n)
        return arrived, run(
            functools.partial(norm_grad, index, len(arrived)), (), (*arrived, parts[0], kept, base, gains),
            [own_f32, ((tokens, D), BF), ((1, D), F32)], [], "norm_grad", 3)

    def sum_pieces(parts):
        total = parts[0]
        for part in chip_reduce(parts[1:], n):
            total = total + part.astype(F32)
        return total

    def pair_sum(left, mine, theirs):
        come = sibling(dot_tn(left, theirs).astype(BF), n)
        return (dot_tn(left, mine) + come.astype(F32)).astype(BF)

    def sum_z(value):
        return lax.psum_scatter(value, "fsdp", scatter_dimension=0, tiled=True)

    def send_z(value):
        parts = [lax.dynamic_index_in_dim(value, level, 0, False)]
        for d in range(1, depth):
            away = lax.dynamic_index_in_dim(value, level ^ d, 0, False)
            parts.append(send(away, "fsdp", depth, lambda i, d=d: i ^ d))
        return parts

    def total_z(parts):
        return sum(part.astype(F32) for part in parts).astype(BF)

    arrived3, (gx2_own, gb2_own, dgain3) = reduce_norm(dh3, 2, x2_own, cotangent[0])
    pair_in = pair_sum(after(h3, *arrived3), dgu, dgu2)
    g_late = after(g, *arrived3)
    come = sibling(dot_tn(act2, g_late).astype(BF), n)
    pair_down = (dot_tn(act, g_late) + come.astype(F32)).astype(BF)[: piece * depth]
    if wide:
        down_rows = pair_down.reshape(depth, piece, D)
        rest = jnp.pad(down_rows[:, :, 2 * units :], ((0, 0), (0, 3 * third - piece), (0, 0)))
        rest = jnp.concatenate([rest[:, t * third : (t + 1) * third] for t in range(3)], axis=2)
        pair = jnp.concatenate([pair_in.reshape(depth, slab, 2 * units), down_rows[:, :, : 2 * units], rest], axis=1)
        grad_units = sum_z(after(pair.reshape(depth * (slab + piece + third), 2 * units), *w_cq))
    else:
        pair = pair_in
        grad_in, grad_down = sum_z(pair_in), sum_z(pair_down)
    gb2_pieces = chip_gather(after(gb2_own, pair, *w_cq), n)
    out_parts = run(
        functools.partial(ffn_output, chips), (place,), (after(act, *gb2_pieces[1:]), act2, down, down2), pieces_out, [full_f32], "ffn_output", 4)
    gb2, dcq, dkv_keep, dkv_away = run(
        functools.partial(cross_grad, chips, heads), (place, corder, *work), (after(wco_rows, pair, *out_parts), cquery, ckey, cvalue, doc_rows, clse, *gb2_pieces),
        [full_bf, rows_bf, ((rows_all // 2, 2 * cols), F32), ((rows_all // 2, 2 * cols), BF)],
        [rows_bf, parted, blocked, ((rows_all, cols), F32), ((rows_all, cols), F32)],
        "cross_grad", 13)
    arrived = chip_reduce(out_parts[1:], n)
    result = after(x2_own, dcq) + out_parts[0]
    for part in arrived:
        result = result + part.astype(F32)
    result = result.astype(BF)
    dcq_pieces = gather_columns(after(dcq, result))
    early = dcq_pieces[1:] or dcq_pieces
    dkv_away = after(dkv_away, *early)
    h2, ocb = lax.optimization_barrier((h2, ocb, *early))[:2]
    ckv_both, *denc = run(
        functools.partial(encoder_grad, chips), (place,), (dkv_keep, sibling(dkv_away, n), wckv, encoder),
        [((D, 2 * cols), BF), ((enc_rows, D), F32), *[((enc_rows, D), BF)] * (chips - 1)], [((rows_all // 2, 2 * cols), BF)],
        "encoder_grad", 7)

    def side_columns(value, parts, mine):
        return part_columns(value, parts, (core if mine else 1 - core) * width, width)

    def middle_of(mine):
        return jnp.concatenate([
            dot_tn(h2, side_columns(dcq, 1, mine)),
            side_columns(ckv_both, 2, mine).astype(F32),
            dot_tn(ocb, columns(gb2, own if mine else other, width)),
        ], axis=1)

    come = sibling(middle_of(False).astype(BF), n)
    middle_pair = (middle_of(True) + come.astype(F32)).astype(BF)
    gb1, dq, dkv_keep, dkv_away, dtable, gx1_own, dgain2 = run(
        functools.partial(self_grad, chips, len(dcq_pieces), len(w_cq), heads, 0), (place, order, corder, zorder),
        (after(x1, *denc, middle_pair, *([grad_units] if wide else [])), gb2, gx2_own, gains, wo_rows, query, key, value, lse, near, starts, places, near_ids, *dcq_pieces, *w_cq),
        [full_bf, rows_bf, ((mine_tokens, 2 * cols), F32), ((mine_tokens, 2 * cols), BF), ((heads, BUCKETS, QB), F32), own_f32, ((1, D), F32)],
        [near_f32, ((1, lanes), F32), full_bf, ((D, D), BF), full_f32, rows_bf, ((stream, 2 * cols), F32), triangle, triangle, ((cols, stream), BF)],
        "self_grad", 15)
    if wide:
        grad_units = lax.all_gather(after(grad_units, dcq_pieces[-1]), "ctx", axis=0)
        middle_pair = after(middle_pair, grad_units, gb1)
    middle = sum_z(middle_pair)
    dqkv, dgain1, *dh1 = run(
        functools.partial(self_close, chips), (place,), (x, dq, dkv_keep, sibling(dkv_away, n), wqkv, *denc[1:]),
        [((mine_tokens, 3 * cols), BF), ((1, D), F32), own_f32, *[((tokens + enc_rows, D), BF)] * (chips - 1)], [full_f32], "self_close", 4)

    dtable = jnp.sum(dtable, axis=2).T
    dtable = jnp.pad(dtable.reshape(depth, per, heads), ((0, 0), (0, 8 - per), (0, 4 * width - heads)))
    dgains = jnp.concatenate([dgain1, jnp.where(chip == 0, dgain2, 0.0), dgain3], axis=0)
    dgains = jnp.transpose(dgains.reshape(3, depth, slab), (1, 0, 2))
    dgains = jnp.pad(dgains, ((0, 0), (0, 5), (0, 4 * width - slab)))

    def last_of(mine):
        return jnp.concatenate([dot_tn(h1, side_columns(dqkv, 3, mine)), dot_tn(ob_all, columns(gb1, own if mine else other, width))], axis=1)

    come = sibling(last_of(False).astype(BF), n)
    last = last_of(True) + come.astype(F32)
    last = jnp.concatenate([last.reshape(depth, slab, 4 * width), dtable, dgains], axis=1).astype(BF)
    last = send_z(last)
    dh1[0] = after(dh1[0], last[1])
    arrived, (grad_hidden, _, _) = reduce_norm(dh1, 0, hidden_in[0], gx1_own)
    grad_enc = denc[0]
    for part in arrived:
        grad_enc = grad_enc + part[tokens:].astype(F32)
    if wide:
        grad_ffn_in, grad_ffn_out = run(
            functools.partial(spread_units, depth, piece), (), (grad_units,), [((slab, 2 * FF), F32), ((n * piece, D), F32)], [], "spread_units", 6)
        grad_cross_q, grad_cross_kv, grad_cross_out = run(
            functools.partial(spread_stacked, 0, (1, 2, 1)), (), (lax.all_gather(after(middle, gb1), "ctx", axis=0),),
            [((slab, D), F32), ((slab, 2 * D), F32), ((slab, D), F32)], [], "spread_stacked", 4)
        last = total_z([after(last[0], grad_hidden, grad_ffn_in), *last[1:]])
        grad_self_qkv, grad_self_out, grad_gains, grad_table = run(
            functools.partial(spread, (3, 1), heads), (order,), ctx_gather(last, n),
            [((slab, 3 * D), F32), ((slab, D), F32), ((3, slab), F32), ((per, H), F32)], [], "spread", 4)
    else:
        def place_columns(pieces, groups):
            outs, first = [], 0
            for g in groups:
                value = pieces[:, :slab, first * width : (first + g) * width].reshape(n, slab, g, width)
                outs.append(jnp.transpose(value, (1, 2, 0, 3)).reshape(slab, g * D).astype(F32))
                first += g
            return outs

        pieces = lax.all_gather(total_z(last), "ctx", axis=0)
        grad_self_qkv, grad_self_out = place_columns(pieces, (3, 1))
        extra = pieces[:, slab:].astype(F32)
        grad_gains = jnp.sum(extra[:, 8:11, :slab], axis=0)
        table = jnp.sum(extra[:, :per, :heads].reshape(chips, 2, per, heads), axis=1)
        grad_table = jnp.transpose(table, (1, 0, 2)).reshape(per, H)
        grad_cross_q, grad_cross_kv, grad_cross_out = place_columns(lax.all_gather(middle, "ctx", axis=0), (1, 2, 1))
        grad_ffn_out = lax.all_gather(grad_down, "ctx", axis=0, tiled=True).astype(F32)
        up_cols = lax.all_gather(grad_in, "ctx", axis=0).reshape(n, slab, 2, units)[..., : piece * depth]
        up_cols = up_cols.reshape(n, slab, 2 * depth, piece)
        grad_ffn_in = jnp.transpose(up_cols, (1, 2, 0, 3)).reshape(slab, 2 * FF).astype(F32)
    return (
        result[None],
        grad_hidden[None],
        grad_enc[None],
        grad_self_qkv,
        grad_self_out,
        grad_table,
        grad_cross_q,
        grad_cross_kv,
        grad_cross_out,
        grad_ffn_in,
        grad_ffn_out,
        grad_gains,
    )


def solution(mesh):
    split = P("fsdp", "ctx", None)
    rows = P("fsdp", None)
    return jax.shard_map(
        body,
        mesh=mesh,
        in_specs=(split, split, rows, rows, split) + (rows,) * 8 + (P(None, "fsdp"),),
        out_specs=(split,) * 3 + (rows,) * 8 + (P(None, "fsdp"),),
        check_vma=False,
    )
```

profile of v0, /device:TPU:0, one launch (start us, length us, event | category | flops | bytes accessed | tf_op | source)
XLA Modules:
  0.0 408.6 jit_solution(15769467545716379448)
XLA Ops:
  13.5 3.1 collective-permute-start
  16.5 2.6 collective-permute-start.4
  24.5 7.0 %collective-permute-done.refs_5_ = bf16[272,640]{1,0:T(8,128)(2,1)} collective-permute-done((bf16[272,640]{1,0:T(8,128)(2,1)S(1)}, bf16[272,640]{1,0:T(8,128)(2,1)}, u32[]{:S(2)}, u32[]{:S(2)}) %collective-permute-start) | collective-permute-done | bytes 348192 | tf_op jit(solution)/shard_map/ppermute | solution.py:47
  33.8 2.8 constant_dynamic-slice_fusion.11
  36.6 7.0 %collective-permute-done.4.refs_6_ = bf16[272,640]{1,0:T(8,128)(2,1)} collective-permute-done((bf16[272,640]{1,0:T(8,128)(2,1)S(1)}, bf16[272,640]{1,0:T(8,128)(2,1)}, u32[]{:S(2)}, u32[]{:S(2)}) %collective-permute-start.4) | collective-permute-done | bytes 348192 | tf_op jit(solution)/shard_map/ppermute | solution.py:47
  48.9 9.9 %collective-permute-done.2.refs_2_ = bf16[128,1024]{1,0:T(8,128)(2,1)S(1)} collective-permute-done((bf16[128,1024]{1,0:T(8,128)(2,1)}, bf16[128,1024]{1,0:T(8,128)(2,1)S(1)}, u32[]{:S(2)}, u32[]{:S(2)}) %collective-permute-start.2) | collective-permute-done | bytes 262176 | tf_op jit(solution)/shard_map/ppermute | solution.py:47
  59.8 6.7 %self_project.1 = (bf16[512,1024]{1,0:T(8,128)(2,1)}, bf16[512,1024]{1,0:T(8,128)(2,1)}, bf16[512,256]{1,0:T(8,128)(2,1)}, bf16[512,512]{1,0:T(8,128)(2,1)}, f32...) custom-call(s32[2]{0:T(128)} %pad_add_fusion.2.place, s32[4]{0:T(128)} %get-tuple-element.258.corder, ...), custom_call_target="tpu_custom_call" | custom-call | flops 1150000000 | bytes 1000000 | tf_op jit(solution)/shard_map/self_project/pallas_call | solution.py:324
  69.6 7.5 %collective-permute-start.10 = (bf16[256,384]{1,0:T(8,128)(2,1)S(1)}, bf16[256,384]{1,0:T(8,128)(2,1)S(1)}, u32[]{:S(2)}, u32[]{:S(2)}) collective-permute-start(bf16[256,384]{1,0:T(8,128)(2,1)S(1)} %copy-done.23), channel_id=1, source_target_pairs={{0,2},{1,3},{2,0},{3,1},{4,6},{5,7},{6,4},{7,5},{8,10},{9,11},{10,... | collective-permute-start | bytes 589832 | tf_op jit(solution)/shard_map/ppermute | solution.py:47
  79.9 6.0 %self_attend.1 = (bf16[1024,256]{1,0:T(8,128)(2,1)}, bf16[1024,256]{1,0:T(8,128)(2,1)}, bf16[512,256]{1,0:T(8,128)(2,1)}, f32[1,2048]{1,0:T(1,128)}) custom-call(s32[2]{0:T(128)} %pad_add_fusion.2.place, bf16[512,256]{1,0:T(8,128)(2,1)} %get-tuple-element.119.q_ref, bf16[512,512]{1,0:T(8,128)(2,1)} %get-tuple-element.121.mine_ref, ...), custom_call_target="tpu_custom_call" | custom-call | flops 1150000000 | bytes 1000000 | tf_op jit(solution)/shard_map/self_attend/pallas_call | solution.py:324
  85.9 5.4 %collective-permute-done.10 = bf16[256,384]{1,0:T(8,128)(2,1)S(1)} collective-permute-done((bf16[256,384]{1,0:T(8,128)(2,1)S(1)}, bf16[256,384]{1,0:T(8,128)(2,1)S(1)}, u32[]{:S(2)}, u32[]{:S(2)}) %collective-permute-start.10) | collective-permute-done | bytes 196640 | tf_op jit(solution)/shard_map/ppermute | solution.py:47
  100.1 8.9 %collective-permute-done.18.refs_5_.refs_9_ = bf16[4,256,256]{2,1,0:T(8,128)(2,1)S(1)} collective-permute-done((bf16[4,256,256]{2,1,0:T(8,128)(2,1)S(1)}, bf16[4,256,256]{2,1,0:T(8,128)(2,1)S(1)}, u32[]{:S(2)}, u32[]{:S(2)}) %collective-permute-start.18) | collective-permute-done | bytes 524320 | tf_op jit(solution)/shard_map/ppermute | solution.py:47
  109.1 2.6 collective-permute-start.20
  112.6 5.1 %encoder_block.1 = (bf16[1024,512]{1,0:T(8,128)(2,1)}, bf16[1024,512]{1,0:T(8,128)(2,1)}) custom-call(s32[2]{0:T(128)} %pad_add_fusion.2.place, s32[4]{0:T(128)} %get-tuple-element.259.zorder, bf16[8,256,1024]{2,1,0:T(8,128)(2,1)} %all-gather.10.cloned.1.call-done.enc_ref, bf16[4,256,384]{2,1,0:T(8,128)(2,1)} %copy-done.14, bf16[4,256,384]{2,1,0:T(8,128)(2,1)} %copy-done.22), custom_call_target="tpu_custom_call" | custom-call | flops 1150000000 | bytes 1000000 | tf_op jit(solution)/shard_map/encoder_block/pallas_call | solution.py:324
  122.6 6.2 %collective-permute-done.17.refs_3_ = bf16[512,256]{1,0:T(8,128)(2,1)} collective-permute-done((bf16[512,256]{1,0:T(8,128)(2,1)}, bf16[512,256]{1,0:T(8,128)(2,1)}, u32[]{:S(2)}, u32[]{:S(2)}) %collective-permute-start.17) | collective-permute-done | bytes 262176 | tf_op jit(solution)/shard_map/ppermute | solution.py:47
  132.8 2.0 collective-permute-start.26
  138.9 15.5 %cross_block.1 = (bf16[2048,256]{1,0:T(8,128)(2,1)}, bf16[2048,256]{1,0:T(8,128)(2,1)}, f32[512,1024]{1,0:T(8,128)}, bf16[512,1024]{1,0:T(8,128)(2,1)}, bf16[512...) custom-call(s32[2]{0:T(128)} %pad_add_fusion.2.place, ...), custom_call_target="tpu_custom_call" | custom-call | flops 6899999744 | bytes 6000000 | tf_op jit(solution)/shard_map/cross_block/pallas_call | solution.py:324
  158.4 5.2 %collective-permute-done.28.refs_5_ = bf16[512,256]{1,0:T(8,128)(2,1)S(1)} collective-permute-done((bf16[512,256]{1,0:T(8,128)(2,1)}, bf16[512,256]{1,0:T(8,128)(2,1)S(1)}, u32[]{:S(2)}, u32[]{:S(2)}) %collective-permute-start.28) | collective-permute-done | bytes 262176 | tf_op jit(solution)/shard_map/ppermute | solution.py:47
  163.6 2.4 collective-permute-done.29.refs_6_
  169.4 2.7 collective-permute-done.31.refs_17_
  173.4 14.0 %ffn_block.1 = (bf16[512,1024]{1,0:T(8,128)(2,1)}, bf16[512,1024]{1,0:T(8,128)(2,1)}, bf16[512,1024]{1,0:T(8,128)(2,1)}, bf16[512,384]{1,0:T(8,128)(2,1)}, bf16[...) custom-call(s32[2]{0:T(128)} %pad_add_fusion.2.place, ...), custom_call_target="tpu_custom_call" | custom-call | flops 16099999744 | bytes 14000000 | tf_op jit(solution)/shard_map/ffn_block/pallas_call | solution.py:324
  188.3 2.0 collective-permute-start.33
  191.0 11.0 %collective-permute-done.32.refs_0_ = bf16[128,1024]{1,0:T(8,128)(2,1)S(1)} collective-permute-done((bf16[128,1024]{1,0:T(8,128)(2,1)}, bf16[128,1024]{1,0:T(8,128)(2,1)S(1)}, u32[]{:S(2)}, u32[]{:S(2)}) %collective-permute-start.32) | collective-permute-done | bytes 262176 | tf_op jit(solution)/shard_map/ppermute | solution.py:47
  202.8 5.0 %collective-permute-done.34.refs_2_ = bf16[128,1024]{1,0:T(8,128)(2,1)S(1)} collective-permute-done((bf16[128,1024]{1,0:T(8,128)(2,1)}, bf16[128,1024]{1,0:T(8,128)(2,1)S(1)}, u32[]{:S(2)}, u32[]{:S(2)}) %collective-permute-start.34) | collective-permute-done | bytes 262176 | tf_op jit(solution)/shard_map/ppermute | solution.py:47
  207.7 2.6 convolution_convert_fusion
  212.3 2.7 collective-permute-done.36
  218.0 2.8 norm_grad.2
  224.3 5.9 %collective-permute-done.37.refs_1_ = bf16[128,1024]{1,0:T(8,128)(2,1)S(1)} collective-permute-done((bf16[128,1024]{1,0:T(8,128)(2,1)}, bf16[128,1024]{1,0:T(8,128)(2,1)S(1)}, u32[]{:S(2)}, u32[]{:S(2)}) %collective-permute-start.37) | collective-permute-done | bytes 262176 | tf_op jit(solution)/shard_map/ppermute | solution.py:47
  230.1 5.9 %collective-permute-done.38.refs_2_ = bf16[128,1024]{1,0:T(8,128)(2,1)S(1)} collective-permute-done((bf16[128,1024]{1,0:T(8,128)(2,1)}, bf16[128,1024]{1,0:T(8,128)(2,1)S(1)}, u32[]{:S(2)}, u32[]{:S(2)}) %collective-permute-start.38) | collective-permute-done | bytes 262176 | tf_op jit(solution)/shard_map/ppermute | solution.py:47
  236.1 4.1 %ffn_output.1 = (f32[128,1024]{1,0:T(8,128)}, bf16[128,1024]{1,0:T(8,128)(2,1)}, bf16[128,1024]{1,0:T(8,128)(2,1)}, bf16[128,1024]{1,0:T(8,128)(2,1)}) custom-call(s32[2]{0:T(128)} %pad_add_fusion.2.place, bf16[512,384]{1,0:T(8,128)(2,1)} %get-tuple-element.152.act0_ref, bf16[512,384]{1,0:T(8,128)(2,1)} %get-tuple-element.147.act1_ref, ...), custom_call_target="tpu_custom_call" | custom-call | flops 4600000000 | bytes 4000000 | tf_op jit(solution)/shard_map/ffn_output/pallas_call | solution.py:324
  243.8 12.7 %cross_grad.1 = (bf16[512,1024]{1,0:T(8,128)(2,1)}, bf16[512,256]{1,0:T(8,128)(2,1)}, f32[1024,512]{1,0:T(8,128)}, bf16[1024,512]{1,0:T(8,128)(2,1)}) custom-call(s32[2]{0:T(128)} %pad_add_fusion.2.place, s32[4]{0:T(128)} %get-tuple-element.258.corder, s32[1]{0:T(128)} %bitcast.19.count_ref, s32[8]{0:T(128)} %copy-done.79, s32[8]{0:T(128)} %copy-done.80, ...), custom_call_target="tpu_custom_call" | custom-call | flops 14949999616 | bytes 13000000 | tf_op jit(solution)/shard_map/cross_grad/pallas_call | solution.py:324
  256.5 2.0 add_convert_fusion.2
  259.6 7.3 %collective-permute-done.45.refs_3_ = bf16[512,256]{1,0:T(8,128)(2,1)S(1)} collective-permute-done((bf16[512,256]{1,0:T(8,128)(2,1)}, bf16[512,256]{1,0:T(8,128)(2,1)S(1)}, u32[]{:S(2)}, u32[]{:S(2)}) %collective-permute-start.45) | collective-permute-done | bytes 262176 | tf_op jit(solution)/shard_map/ppermute | solution.py:47
  269.8 4.0 collective-permute-done.43.refs_1_
  278.6 7.0 %encoder_grad.1 = (bf16[1024,512]{1,0:T(8,128)(2,1)}, f32[256,1024]{1,0:T(8,128)}, bf16[256,1024]{1,0:T(8,128)(2,1)}, bf16[256,1024]{1,0:T(8,128)(2,1)}, bf16[256,1024]{1,0:T(8,128)(2,1)}) custom-call(s32[2]{0:T(128)} %pad_add_fusion.2.place, f32[1024,512]{1,0:T(8,128)} %get-tuple-element.166.keep_ref, bf16[1024,512]{1,0:T(8,128)(2,1)} %collective-permute-done.46.come_ref, ...), custom_call_target="tpu_custom_call" | custom-call | flops 8049999872 | bytes 7000000 | tf_op jit(solution)/shard_map/encoder_grad/pallas_call | solution.py:324
  285.6 2.0 constant_dynamic-slice_fusion.8
  292.1 2.5 fusion.3
  294.5 14.8 %self_grad.1 = (bf16[512,1024]{1,0:T(8,128)(2,1)}, bf16[512,256]{1,0:T(8,128)(2,1)}, f32[512,512]{1,0:T(8,128)}, bf16[512,512]{1,0:T(8,128)(2,1)}, f32[4,32,128]...) custom-call(s32[2]{0:T(128)} %pad_add_fusion.2.place, s32[8]{0:T(128)} %stack.105.order, ...), custom_call_target="tpu_custom_call" | custom-call | flops 17250000896 | bytes 15000000 | tf_op jit(solution)/shard_map/self_grad/pallas_call | solution.py:324
  312.3 5.6 %self_close.1 = (bf16[512,768]{1,0:T(8,128)(2,1)}, f32[1,1024]{1,0:T(1,128)}, f32[128,1024]{1,0:T(8,128)}, bf16[384,1024]{1,0:T(8,128)(2,1)}, bf16[384,1024]{1,0:T(8,128)(2,1)}, /*index=5*/bf16[384,1024]{1,0:T(8,128)(2,1)}) custom-call(s32[2]{0:T(128)} %pad_add_fusion.2.place, bf16[512,1024]{1,0:T(8,128)(2,1)} %get-tuple-element.117.x_ref, ...), custom_call_target="tpu_custom_call" | custom-call | flops 4600000000 | bytes 4000000 | tf_op jit(solution)/shard_map/self_close/pallas_call | solution.py:324
  326.2 9.6 %reduce-scatter.5.cloned.1.call-done = bf16[256,512]{1,0:T(8,128)(2,1)} async-done(((bf16[1024,512]{1,0:T(8,128)(2,1)}), bf16[256,512]{1,0:T(8,128)(2,1)}) %reduce-scatter.5.cloned.1.call-update) | async-done | bytes 262160 | tf_op jit(solution)/shard_map/reduce_scatter | solution.py:930
  340.5 12.4 %collective-permute-done.53 = bf16[272,512]{1,0:T(8,128)(2,1)S(1)} collective-permute-done((bf16[272,512]{1,0:T(8,128)(2,1)S(1)}, bf16[272,512]{1,0:T(8,128)(2,1)S(1)}, u32[]{:S(2)}, u32[]{:S(2)}) %collective-permute-start.53) | collective-permute-done | bytes 278560 | tf_op jit(solution)/shard_map/ppermute | solution.py:47
  353.2 10.4 %collective-permute-done.51.refs_2_ = bf16[384,1024]{1,0:T(8,128)(2,1)} collective-permute-done((bf16[384,1024]{1,0:T(8,128)(2,1)}, bf16[384,1024]{1,0:T(8,128)(2,1)}, u32[]{:S(2)}, u32[]{:S(2)}) %collective-permute-start.51) | collective-permute-done | bytes 786464 | tf_op jit(solution)/shard_map/ppermute | solution.py:47
  363.6 3.2 norm_grad.3
  366.8 7.4 %spread_units.1 = (f32[256,5632]{1,0:T(8,128)}, f32[704,1024]{1,0:T(8,128)}) custom-call(bf16[8,376,768]{2,1,0:T(8,128)(2,1)} %bitcast.116), custom_call_target="tpu_custom_call" | custom-call | flops 6899999744 | bytes 6000000 | tf_op jit(solution)/shard_map/spread_units/pallas_call | solution.py:324
  376.6 6.3 %collective-permute-done.56.refs_1_ = bf16[272,512]{1,0:T(8,128)(2,1)S(1)} collective-permute-done((bf16[272,512]{1,0:T(8,128)(2,1)S(1)}, bf16[272,512]{1,0:T(8,128)(2,1)S(1)}, u32[]{:S(2)}, u32[]{:S(2)}) %collective-permute-start.56) | collective-permute-done | bytes 278560 | tf_op jit(solution)/shard_map/ppermute | solution.py:47
  385.3 4.1 %collective-permute-done.58.refs_3_ = bf16[272,512]{1,0:T(8,128)(2,1)S(1)} collective-permute-done((bf16[272,512]{1,0:T(8,128)(2,1)S(1)}, bf16[272,512]{1,0:T(8,128)(2,1)S(1)}, u32[]{:S(2)}, u32[]{:S(2)}) %collective-permute-start.58) | collective-permute-done | bytes 278560 | tf_op jit(solution)/shard_map/ppermute | solution.py:47
  389.5 2.8 add_bitcast_fusion
  393.8 3.8 spread.1
  397.7 3.9 spread_stacked.1
  (375 shorter events, 106.7 us)
Async XLA Ops:
  7.2 104.5 %all-gather.10.cloned.1.call-start = ((), (), s32[]{:S(2)}) async-start(), calls=%async_computation.2 | async-start | bytes 4718592 | tf_op jit(solution)/shard_map/all_gather | solution.py:803
  7.9 150.4 %all-gather.12.cloned.1.call-start = ((), (), s32[]{:S(2)}) async-start(), calls=%async_computation.5 | async-start | bytes 2887680 | tf_op jit(solution)/shard_map/all_gather | solution.py:890
  13.5 18.0 %collective-permute-start = (bf16[272,640]{1,0:T(8,128)(2,1)S(1)}, bf16[272,640]{1,0:T(8,128)(2,1)}, u32[]{:S(2)}, u32[]{:S(2)}) collective-permute-start(bf16[272,640]{1,0:T(8,128)(2,1)S(1)} %first_weights.2.refs_4_), channel_id=1, source_target_pairs={{0,1},{1,0},{2,3},{3,2},{4,5},{5,4},{6,7},{7,6},{8,9},{9,8},{10,11... | collective-permute-start | bytes 1044488 | tf_op jit(solution)/shard_map/ppermute | solution.py:47
  16.5 27.0 %collective-permute-start.4 = (bf16[272,640]{1,0:T(8,128)(2,1)S(1)}, bf16[272,640]{1,0:T(8,128)(2,1)}, u32[]{:S(2)}, u32[]{:S(2)}) collective-permute-start(bf16[272,640]{1,0:T(8,128)(2,1)S(1)} %first_weights.2.refs_4_), channel_id=1, source_target_pairs={{0,2},{1,3},{2,0},{3,1},{4,6},{5,7},{6,4},{7,5},{8,10},{9,11},{10,... | collective-permute-start | bytes 1044488 | tf_op jit(solution)/shard_map/ppermute | solution.py:47
  19.1 24.4 %collective-permute-start.5 = (bf16[272,640]{1,0:T(8,128)(2,1)S(1)}, bf16[272,640]{1,0:T(8,128)(2,1)}, u32[]{:S(2)}, u32[]{:S(2)}) collective-permute-start(bf16[272,640]{1,0:T(8,128)(2,1)S(1)} %first_weights.2.refs_4_), channel_id=1, source_target_pairs={{0,3},{1,2},{2,1},{3,0},{4,7},{5,6},{6,5},{7,4},{8,11},{9,10},{10,... | collective-permute-start | bytes 1044488 | tf_op jit(solution)/shard_map/ppermute | solution.py:47
  31.5 14.7 %collective-permute-start.1 = (bf16[128,1024]{1,0:T(8,128)(2,1)}, bf16[128,1024]{1,0:T(8,128)(2,1)}, u32[]{:S(2)}, u32[]{:S(2)}) collective-permute-start(bf16[128,1024]{1,0:T(8,128)(2,1)} %bitcast.126), channel_id=1, source_target_pairs={{0,8},{4,12},{8,0},{12,4},{16,24},{20,28},{24,16},{28,20},{1,9},{5... | collective-permute-start | bytes 786440 | tf_op jit(solution)/shard_map/ppermute | solution.py:47
  36.6 22.3 %collective-permute-start.6 = (bf16[272,640]{1,0:T(8,128)(2,1)}, bf16[272,640]{1,0:T(8,128)(2,1)S(1)}, u32[]{:S(2)}, u32[]{:S(2)}) collective-permute-start(bf16[272,640]{1,0:T(8,128)(2,1)} %collective-permute-done.refs_5_), channel_id=1, source_target_pairs={{0,4},{4,0},{8,12},{12,8},{16,20},{20,16},{24,28},{28,24},{1,5},{5... | collective-permute-start | bytes 1044488 | tf_op jit(solution)/shard_map/ppermute | solution.py:47
  43.5 15.4 %collective-permute-start.7 = (bf16[272,640]{1,0:T(8,128)(2,1)}, bf16[272,640]{1,0:T(8,128)(2,1)}, u32[]{:S(2)}, u32[]{:S(2)}) collective-permute-start(bf16[272,640]{1,0:T(8,128)(2,1)} %collective-permute-done.4.refs_6_), channel_id=1, source_target_pairs={{0,4},{4,0},{8,12},{12,8},{16,20},{20,16},{24,28},{28,24},{1,5},{5... | collective-permute-start | bytes 1044488 | tf_op jit(solution)/shard_map/ppermute | solution.py:47
  43.6 15.4 %collective-permute-start.8 = (bf16[272,640]{1,0:T(8,128)(2,1)}, bf16[272,640]{1,0:T(8,128)(2,1)}, u32[]{:S(2)}, u32[]{:S(2)}) collective-permute-start(bf16[272,640]{1,0:T(8,128)(2,1)} %collective-permute-done.5.refs_7_), channel_id=1, source_target_pairs={{0,4},{4,0},{8,12},{12,8},{16,20},{20,16},{24,28},{28,24},{1,5},{5... | collective-permute-start | bytes 1044488 | tf_op jit(solution)/shard_map/ppermute | solution.py:47
  44.7 14.2 %collective-permute-start.2 = (bf16[128,1024]{1,0:T(8,128)(2,1)}, bf16[128,1024]{1,0:T(8,128)(2,1)S(1)}, u32[]{:S(2)}, u32[]{:S(2)}) collective-permute-start(bf16[128,1024]{1,0:T(8,128)(2,1)} %bitcast.127), channel_id=1, source_target_pairs={{0,16},{4,20},{8,24},{12,28},{16,0},{20,4},{24,8},{28,12},{1,17},{... | collective-permute-start | bytes 786440 | tf_op jit(solution)/shard_map/ppermute | solution.py:47
  46.2 12.7 %collective-permute-start.3 = (bf16[128,1024]{1,0:T(8,128)(2,1)}, bf16[128,1024]{1,0:T(8,128)(2,1)S(1)}, u32[]{:S(2)}, u32[]{:S(2)}) collective-permute-start(bf16[128,1024]{1,0:T(8,128)(2,1)} %bitcast.128), channel_id=1, source_target_pairs={{0,24},{4,28},{8,16},{12,20},{16,8},{20,12},{24,0},{28,4},{1,25},{... | collective-permute-start | bytes 786440 | tf_op jit(solution)/shard_map/ppermute | solution.py:47
  66.6 12.5 %collective-permute-start.12 = (bf16[512,512]{1,0:T(8,128)(2,1)}, bf16[512,512]{1,0:T(8,128)(2,1)S(1)}, u32[]{:S(2)}, u32[]{:S(2)}) collective-permute-start(bf16[512,512]{1,0:T(8,128)(2,1)} %get-tuple-element.121.mine_ref), channel_id=1, source_target_pairs={{0,4},{4,0},{8,12},{12,8},{16,20},{20,16},{24,28},{28,24},{1,5},{5... | collective-permute-start | bytes 1572872 | tf_op jit(solution)/shard_map/ppermute | solution.py:47
  69.6 21.7 %collective-permute-start.10 = (bf16[256,384]{1,0:T(8,128)(2,1)S(1)}, bf16[256,384]{1,0:T(8,128)(2,1)S(1)}, u32[]{:S(2)}, u32[]{:S(2)}) collective-permute-start(bf16[256,384]{1,0:T(8,128)(2,1)S(1)} %copy-done.23), channel_id=1, source_target_pairs={{0,2},{1,3},{2,0},{3,1},{4,6},{5,7},{6,4},{7,5},{8,10},{9,11},{10,... | collective-permute-start | bytes 589832 | tf_op jit(solution)/shard_map/ppermute | solution.py:47
  77.1 14.2 %collective-permute-start.11 = (bf16[256,384]{1,0:T(8,128)(2,1)S(1)}, bf16[256,384]{1,0:T(8,128)(2,1)S(1)}, u32[]{:S(2)}, u32[]{:S(2)}) collective-permute-start(bf16[256,384]{1,0:T(8,128)(2,1)S(1)} %copy-done.23), channel_id=1, source_target_pairs={{0,3},{1,2},{2,1},{3,0},{4,7},{5,6},{6,5},{7,4},{8,11},{9,10},{10,... | collective-permute-start | bytes 589832 | tf_op jit(solution)/shard_map/ppermute | solution.py:47
  78.5 14.0 %collective-permute-start.9 = (bf16[256,384]{1,0:T(8,128)(2,1)S(1)}, bf16[256,384]{1,0:T(8,128)(2,1)S(1)}, u32[]{:S(2)}, u32[]{:S(2)}) collective-permute-start(bf16[256,384]{1,0:T(8,128)(2,1)S(1)} %copy-done.23), channel_id=1, source_target_pairs={{0,1},{1,0},{2,3},{3,2},{4,5},{5,4},{6,7},{7,6},{8,9},{9,8},{10,11... | collective-permute-start | bytes 589832 | tf_op jit(solution)/shard_map/ppermute | solution.py:47
  92.6 125.3 %all-gather.14.cloned.1.call-start = ((), (), s32[]{:S(2)}) async-start(), calls=%async_computation.6 | async-start | bytes 2359296 | tf_op jit(solution)/shard_map/all_gather | solution.py:911
  95.0 16.7 %collective-permute-start.13 = (bf16[4,256,384]{2,1,0:T(8,128)(2,1)S(1)}, bf16[4,256,384]{2,1,0:T(8,128)(2,1)S(1)}, u32[]{:S(2)}, u32[]{:S(2)}) collective-permute-start(bf16[4,256,384]{2,1,0:T(8,128)(2,1)S(1)} %pad_maximum_fusion.2.refs_0_.refs_12_), channel_id=1, source_target_pairs={{0,4},{4,0},{8,12},{12,8},{16,20},{20,16},{24,28},{28,24},{1,5},{5... | collective-permute-start | bytes 2359304 | tf_op jit(solution)/shard_map/ppermute | solution.py:47
  96.1 13.0 %collective-permute-start.18 = (bf16[4,256,256]{2,1,0:T(8,128)(2,1)S(1)}, bf16[4,256,256]{2,1,0:T(8,128)(2,1)S(1)}, u32[]{:S(2)}, u32[]{:S(2)}) collective-permute-start(bf16[4,256,256]{2,1,0:T(8,128)(2,1)S(1)} %pad_maximum_fusion.3.refs_4_.refs_8_), channel_id=1, source_target_pairs={{0,8},{4,20},{8,0},{12,28},{16,24},{20,4},{24,16},{28,12},{1,9},{5... | collective-permute-start | bytes 1572872 | tf_op jit(solution)/shard_map/ppermute | solution.py:47
  98.6 19.7 %collective-permute-start.19 = (bf16[4,256,256]{2,1,0:T(8,128)(2,1)S(1)}, bf16[4,256,256]{2,1,0:T(8,128)(2,1)S(1)}, u32[]{:S(2)}, u32[]{:S(2)}) collective-permute-start(bf16[4,256,256]{2,1,0:T(8,128)(2,1)S(1)} %pad_maximum_fusion.3.refs_4_.refs_8_), channel_id=1, source_target_pairs={{0,16},{4,12},{8,24},{12,4},{16,0},{20,28},{24,8},{28,20},{1,17},{... | collective-permute-start | bytes 1572872 | tf_op jit(solution)/shard_map/ppermute | solution.py:47
  100.1 20.6 %collective-permute-start.21 = (bf16[4,256,256]{2,1,0:T(8,128)(2,1)S(1)}, bf16[4,256,256]{2,1,0:T(8,128)(2,1)}, u32[]{:S(2)}, u32[]{:S(2)}) collective-permute-start(bf16[4,256,256]{2,1,0:T(8,128)(2,1)S(1)} %pad_maximum_fusion.3.refs_4_.refs_8_), channel_id=1, source_target_pairs={{0,4},{4,0},{8,12},{12,8},{16,20},{20,16},{24,28},{28,24},{1,5},{5... | collective-permute-start | bytes 1572872 | tf_op jit(solution)/shard_map/ppermute | solution.py:47
  109.1 11.7 %collective-permute-start.20 = (bf16[4,256,256]{2,1,0:T(8,128)(2,1)S(1)}, bf16[4,256,256]{2,1,0:T(8,128)(2,1)}, u32[]{:S(2)}, u32[]{:S(2)}) collective-permute-start(bf16[4,256,256]{2,1,0:T(8,128)(2,1)S(1)} %collective-permute-done.18.refs_5_.refs_9_), channel_id=1, source_target_pairs={{0,16},{4,12},{8,24},{12,4},{16,0},{20,28},{24,8},{28,20},{1,17},{... | collective-permute-start | bytes 1572872 | tf_op jit(solution)/shard_map/ppermute | solution.py:47
  117.7 19.5 %collective-permute-start.14 = (bf16[1024,512]{1,0:T(8,128)(2,1)}, bf16[1024,512]{1,0:T(8,128)(2,1)S(1)}, u32[]{:S(2)}, u32[]{:S(2)}) collective-permute-start(bf16[1024,512]{1,0:T(8,128)(2,1)} %get-tuple-element.128.kvm_ref), channel_id=1, source_target_pairs={{0,4},{4,0},{8,12},{12,8},{16,20},{20,16},{24,28},{28,24},{1,5},{5... | collective-permute-start | bytes 3145736 | tf_op jit(solution)/shard_map/ppermute | solution.py:47
  118.3 10.4 %collective-permute-start.17 = (bf16[512,256]{1,0:T(8,128)(2,1)}, bf16[512,256]{1,0:T(8,128)(2,1)}, u32[]{:S(2)}, u32[]{:S(2)}) collective-permute-start(bf16[512,256]{1,0:T(8,128)(2,1)} %get-tuple-element.123.refs_0_), channel_id=1, source_target_pairs={{0,24},{4,28},{8,16},{12,20},{16,8},{20,12},{24,0},{28,4},{1,25},{... | collective-permute-start | bytes 786440 | tf_op jit(solution)/shard_map/ppermute | solution.py:47
  120.7 16.4 %collective-permute-start.24 = (bf16[4,256,256]{2,1,0:T(8,128)(2,1)}, bf16[4,256,256]{2,1,0:T(8,128)(2,1)S(1)}, u32[]{:S(2)}, u32[]{:S(2)}) collective-permute-start(bf16[4,256,256]{2,1,0:T(8,128)(2,1)} %collective-permute-done.20.refs_7_.refs_11_), channel_id=1, source_target_pairs={{0,4},{4,0},{8,12},{12,8},{16,20},{20,16},{24,28},{28,24},{1,5},{5... | collective-permute-start | bytes 1572872 | tf_op jit(solution)/shard_map/ppermute | solution.py:47
  121.3 11.5 %collective-permute-start.15 = (bf16[512,256]{1,0:T(8,128)(2,1)}, bf16[512,256]{1,0:T(8,128)(2,1)S(1)}, u32[]{:S(2)}, u32[]{:S(2)}) collective-permute-start(bf16[512,256]{1,0:T(8,128)(2,1)} %get-tuple-element.123.refs_0_), channel_id=1, source_target_pairs={{0,8},{4,12},{8,0},{12,4},{16,24},{20,28},{24,16},{28,20},{1,9},{5... | collective-permute-start | bytes 786440 | tf_op jit(solution)/shard_map/ppermute | solution.py:47
  129.4 25.0 %collective-permute-start.25 = (bf16[128,1024]{1,0:T(8,128)(2,1)}, bf16[128,1024]{1,0:T(8,128)(2,1)}, u32[]{:S(2)}, u32[]{:S(2)}) collective-permute-start(bf16[128,1024]{1,0:T(8,128)(2,1)} %bitcast.121), channel_id=1, source_target_pairs={{0,8},{4,12},{8,0},{12,4},{16,24},{20,28},{24,16},{28,20},{1,9},{5... | collective-permute-start | bytes 786440 | tf_op jit(solution)/shard_map/ppermute | solution.py:47
  132.8 21.6 %collective-permute-start.26 = (bf16[128,1024]{1,0:T(8,128)(2,1)}, bf16[128,1024]{1,0:T(8,128)(2,1)}, u32[]{:S(2)}, u32[]{:S(2)}) collective-permute-start(bf16[128,1024]{1,0:T(8,128)(2,1)} %bitcast.122), channel_id=1, source_target_pairs={{0,16},{4,20},{8,24},{12,28},{16,0},{20,4},{24,8},{28,12},{1,17},{... | collective-permute-start | bytes 786440 | tf_op jit(solution)/shard_map/ppermute | solution.py:47
  136.2 18.3 %collective-permute-start.27 = (bf16[128,1024]{1,0:T(8,128)(2,1)}, bf16[128,1024]{1,0:T(8,128)(2,1)}, u32[]{:S(2)}, u32[]{:S(2)}) collective-permute-start(bf16[128,1024]{1,0:T(8,128)(2,1)} %bitcast.123), channel_id=1, source_target_pairs={{0,24},{4,28},{8,16},{12,20},{16,8},{20,12},{24,0},{28,4},{1,25},{... | collective-permute-start | bytes 786440 | tf_op jit(solution)/shard_map/ppermute | solution.py:47
  155.5 10.5 %collective-permute-start.29 = (bf16[512,256]{1,0:T(8,128)(2,1)}, bf16[512,256]{1,0:T(8,128)(2,1)S(1)}, u32[]{:S(2)}, u32[]{:S(2)}) collective-permute-start(bf16[512,256]{1,0:T(8,128)(2,1)} %get-tuple-element.132.refs_4_), channel_id=1, source_target_pairs={{0,16},{4,20},{8,24},{12,28},{16,0},{20,4},{24,8},{28,12},{1,17},{... | collective-permute-start | bytes 786440 | tf_op jit(solution)/shard_map/ppermute | solution.py:47
  169.1 97.8 %reduce-scatter.3.cloned.1.call-start = ((), (), s32[]{:S(2)}) async-start(), calls=%async_computation.3 | async-start | bytes 2887680 | tf_op jit(solution)/shard_map/reduce_scatter | solution.py:930
  187.4 14.6 %collective-permute-start.32 = (bf16[128,1024]{1,0:T(8,128)(2,1)}, bf16[128,1024]{1,0:T(8,128)(2,1)S(1)}, u32[]{:S(2)}, u32[]{:S(2)}) collective-permute-start(bf16[128,1024]{1,0:T(8,128)(2,1)} %get-tuple-element.138), channel_id=1, source_target_pairs={{0,8},{4,12},{8,0},{12,4},{16,24},{20,28},{24,16},{28,20},{1,9},{5... | collective-permute-start | bytes 786440 | tf_op jit(solution)/shard_map/ppermute | solution.py:47
  188.3 14.5 %collective-permute-start.33 = (bf16[128,1024]{1,0:T(8,128)(2,1)}, bf16[128,1024]{1,0:T(8,128)(2,1)S(1)}, u32[]{:S(2)}, u32[]{:S(2)}) collective-permute-start(bf16[128,1024]{1,0:T(8,128)(2,1)} %get-tuple-element.139), channel_id=1, source_target_pairs={{0,16},{4,20},{8,24},{12,28},{16,0},{20,4},{24,8},{28,12},{1,17},{... | collective-permute-start | bytes 786440 | tf_op jit(solution)/shard_map/ppermute | solution.py:47
  190.2 17.5 %collective-permute-start.34 = (bf16[128,1024]{1,0:T(8,128)(2,1)}, bf16[128,1024]{1,0:T(8,128)(2,1)S(1)}, u32[]{:S(2)}, u32[]{:S(2)}) collective-permute-start(bf16[128,1024]{1,0:T(8,128)(2,1)} %get-tuple-element.140), channel_id=1, source_target_pairs={{0,24},{4,28},{8,16},{12,20},{16,8},{20,12},{24,0},{28,4},{1,25},{... | collective-permute-start | bytes 786440 | tf_op jit(solution)/shard_map/ppermute | solution.py:47
  217.9 91.6 %all-gather.16.cloned.1.call-start = ((), (), s32[]{:S(2)}) async-start(), calls=%async_computation.7 | async-start | bytes 5197824 | tf_op jit(solution)/shard_map/all_gather | solution.py:997
  222.2 13.9 %collective-permute-start.38 = (bf16[128,1024]{1,0:T(8,128)(2,1)}, bf16[128,1024]{1,0:T(8,128)(2,1)S(1)}, u32[]{:S(2)}, u32[]{:S(2)}) collective-permute-start(bf16[128,1024]{1,0:T(8,128)(2,1)} %get-tuple-element.151.refs_0_), channel_id=1, source_target_pairs={{0,16},{4,20},{8,24},{12,28},{16,0},{20,4},{24,8},{28,12},{1,17},{... | collective-permute-start | bytes 786440 | tf_op jit(solution)/shard_map/ppermute | solution.py:47
  222.8 13.2 %collective-permute-start.39 = (bf16[128,1024]{1,0:T(8,128)(2,1)}, bf16[128,1024]{1,0:T(8,128)(2,1)S(1)}, u32[]{:S(2)}, u32[]{:S(2)}) collective-permute-start(bf16[128,1024]{1,0:T(8,128)(2,1)} %get-tuple-element.151.refs_0_), channel_id=1, source_target_pairs={{0,24},{4,28},{8,16},{12,20},{16,8},{20,12},{24,0},{28,4},{1,25},{... | collective-permute-start | bytes 786440 | tf_op jit(solution)/shard_map/ppermute | solution.py:47
  240.2 16.3 %collective-permute-start.40 = (bf16[128,1024]{1,0:T(8,128)(2,1)}, bf16[128,1024]{1,0:T(8,128)(2,1)S(1)}, u32[]{:S(2)}, u32[]{:S(2)}) collective-permute-start(bf16[128,1024]{1,0:T(8,128)(2,1)} %get-tuple-element.156), channel_id=1, source_target_pairs={{0,8},{4,12},{8,0},{12,4},{16,24},{20,28},{24,16},{28,20},{1,9},{5... | collective-permute-start | bytes 786440 | tf_op jit(solution)/shard_map/ppermute | solution.py:47
  241.0 15.5 %collective-permute-start.41 = (bf16[128,1024]{1,0:T(8,128)(2,1)}, bf16[128,1024]{1,0:T(8,128)(2,1)S(1)}, u32[]{:S(2)}, u32[]{:S(2)}) collective-permute-start(bf16[128,1024]{1,0:T(8,128)(2,1)} %get-tuple-element.157), channel_id=1, source_target_pairs={{0,16},{4,20},{8,24},{12,28},{16,0},{20,4},{24,8},{28,12},{1,17},{... | collective-permute-start | bytes 786440 | tf_op jit(solution)/shard_map/ppermute | solution.py:47
  241.9 14.6 %collective-permute-start.42 = (bf16[128,1024]{1,0:T(8,128)(2,1)}, bf16[128,1024]{1,0:T(8,128)(2,1)}, u32[]{:S(2)}, u32[]{:S(2)}) collective-permute-start(bf16[128,1024]{1,0:T(8,128)(2,1)} %get-tuple-element.158), channel_id=1, source_target_pairs={{0,24},{4,28},{8,16},{12,20},{16,8},{20,12},{24,0},{28,4},{1,25},{... | collective-permute-start | bytes 786440 | tf_op jit(solution)/shard_map/ppermute | solution.py:47
  266.9 68.9 %reduce-scatter.5.cloned.1.call-start = ((), (), s32[]{:S(2)}) async-start(), calls=%async_computation.4 | async-start | bytes 1310720 | tf_op jit(solution)/shard_map/reduce_scatter | solution.py:930
  309.6 88.1 %all-gather.18.cloned.1.call-start = ((), (), s32[]{:S(2)}) async-start(), calls=%async_computation.8 | async-start | bytes 2359296 | tf_op jit(solution)/shard_map/all_gather | solution.py:1026
  320.9 15.5 %collective-permute-start.52 = (bf16[1024,512]{0,1:T(8,128)(2,1)}, bf16[1024,512]{0,1:T(8,128)(2,1)}, u32[]{:S(2)}, u32[]{:S(2)}) collective-permute-start(bf16[1024,512]{0,1:T(8,128)(2,1)} %pad_maximum_fusion.1), channel_id=1, source_target_pairs={{0,4},{4,0},{8,12},{12,8},{16,20},{20,16},{24,28},{28,24},{1,5},{5... | collective-permute-start | bytes 3145736 | tf_op jit(solution)/shard_map/ppermute | solution.py:47
  322.6 30.5 %collective-permute-start.49 = (bf16[384,1024]{1,0:T(8,128)(2,1)}, bf16[384,1024]{1,0:T(8,128)(2,1)}, u32[]{:S(2)}, u32[]{:S(2)}) collective-permute-start(bf16[384,1024]{1,0:T(8,128)(2,1)} %get-tuple-element.192), channel_id=1, source_target_pairs={{0,8},{4,12},{8,0},{12,4},{16,24},{20,28},{24,16},{28,20},{1,9},{5... | collective-permute-start | bytes 2359304 | tf_op jit(solution)/shard_map/ppermute | solution.py:47
  322.7 30.4 %collective-permute-start.50 = (bf16[384,1024]{1,0:T(8,128)(2,1)}, bf16[384,1024]{1,0:T(8,128)(2,1)}, u32[]{:S(2)}, u32[]{:S(2)}) collective-permute-start(bf16[384,1024]{1,0:T(8,128)(2,1)} %get-tuple-element.193), channel_id=1, source_target_pairs={{0,16},{4,20},{8,24},{12,28},{16,0},{20,4},{24,8},{28,12},{1,17},{... | collective-permute-start | bytes 2359304 | tf_op jit(solution)/shard_map/ppermute | solution.py:47
  324.5 39.1 %collective-permute-start.51 = (bf16[384,1024]{1,0:T(8,128)(2,1)}, bf16[384,1024]{1,0:T(8,128)(2,1)}, u32[]{:S(2)}, u32[]{:S(2)}) collective-permute-start(bf16[384,1024]{1,0:T(8,128)(2,1)} %get-tuple-element.194), channel_id=1, source_target_pairs={{0,24},{4,28},{8,16},{12,20},{16,8},{20,12},{24,0},{28,4},{1,25},{... | collective-permute-start | bytes 2359304 | tf_op jit(solution)/shard_map/ppermute | solution.py:47
  338.8 14.0 %collective-permute-start.53 = (bf16[272,512]{1,0:T(8,128)(2,1)S(1)}, bf16[272,512]{1,0:T(8,128)(2,1)S(1)}, u32[]{:S(2)}, u32[]{:S(2)}) collective-permute-start(bf16[272,512]{1,0:T(8,128)(2,1)S(1)} %get-tuple-element.237), channel_id=1, source_target_pairs={{0,1},{1,0},{2,3},{3,2},{4,5},{5,4},{6,7},{7,6},{8,9},{9,8},{10,11... | collective-permute-start | bytes 835592 | tf_op jit(solution)/shard_map/ppermute | solution.py:47
  338.9 35.3 %collective-permute-start.54 = (bf16[272,512]{1,0:T(8,128)(2,1)S(1)}, bf16[272,512]{1,0:T(8,128)(2,1)S(1)}, u32[]{:S(2)}, u32[]{:S(2)}) collective-permute-start(bf16[272,512]{1,0:T(8,128)(2,1)S(1)} %get-tuple-element.236), channel_id=1, source_target_pairs={{0,2},{1,3},{2,0},{3,1},{4,6},{5,7},{6,4},{7,5},{8,10},{9,11},{10,... | collective-permute-start | bytes 835592 | tf_op jit(solution)/shard_map/ppermute | solution.py:47
  352.9 21.4 %collective-permute-start.55 = (bf16[272,512]{1,0:T(8,128)(2,1)S(1)}, bf16[272,512]{1,0:T(8,128)(2,1)S(1)}, u32[]{:S(2)}, u32[]{:S(2)}) collective-permute-start(bf16[272,512]{1,0:T(8,128)(2,1)S(1)} %get-tuple-element.235), channel_id=1, source_target_pairs={{0,3},{1,2},{2,1},{3,0},{4,7},{5,6},{6,5},{7,4},{8,11},{9,10},{10,... | collective-permute-start | bytes 835592 | tf_op jit(solution)/shard_map/ppermute | solution.py:47
  (106 other events, 949.9 us)
Sparse Core Ops, SparseCore 0:
  9.9 43.4 all-gather.9
  92.7 50.7 all-gather.11
  169.2 34.7 all-gather.13
  218.1 46.4 reduce-scatter.2
  267.0 37.8 all-gather.15
  309.7 26.0 reduce-scatter.4
  337.7 38.3 all-gather.17
where the time goes:
time: 417 us; the launch traced here: 409 us
  waiting for transfers between devices  151 us (36%)
  Pallas kernels  114 us (27%)
  starting transfers between devices  64.1 us (15%)
  local copies, waits for them, and re-layouts  33.8 us (8%)
  other arithmetic  17.5 us (4%)
  between operations  15.6 us (4%)
  matrix products  13.3 us (3%)
    ppermute x63, waiting for transfers between devices, send(): return lax.ppermute(value, axis, [(i, target(i)) for i in range(count)])  140 us
    pallas_call x15, Pallas kernels, run(): pl.pallas_call(kernel, in_specs=[smem] * len(scalars) + [vmem] * len(arra...  113 us
    ppermute x63, starting transfers between devices, send(): return lax.ppermute(value, axis, [(i, target(i)) for i in range(count)])  62.8 us
    unnamed x169, local copies, waits for them, and re-layouts  14.6 us
    dot_general x12, matrix products, dot_tn(): lax.dot_general(a, b, (((0,), (0,)), ((), ())), preferred_element_type=F32)  13.3 us
    reduce_scatter x2, waiting for transfers between devices, sum_z(): return lax.psum_scatter(value, 'fsdp', scatter_dimension=0, tiled=True)  9.6 us
  transfers between devices with their start and end apart: 70, of which 30 were waited for; matrix products, arithmetic and copies ran while one was open for 12% of the time, Pallas kernels for 27%

commit v1 on v0

--- a/solution.py
+++ b/solution.py
@@ -994,7 +994,7 @@
         [near_f32, ((1, lanes), F32), full_bf, ((D, D), BF), full_f32, rows_bf, ((stream, 2 * cols), F32), triangle, triangle, ((cols, stream), BF)],
         "self_grad", 15)
     if wide:
-        grad_units = lax.all_gather(after(grad_units, dcq_pieces[-1]), "ctx", axis=0)
+        grad_units = lax.all_gather(after(grad_units, *dcq_pieces[1:]), "ctx", axis=0)
         middle_pair = after(middle_pair, grad_units, gb1)
     middle = sum_z(middle_pair)
     dqkv, dgain1, *dh1 = run(

time: 417 us -> 417 us (level)
    ppermute x63, waiting for transfers between devices: 140 us -> 131 us  [send(): return lax.ppermute(value, axis, [(i, target(i)) for i in range(count)])]
    all_gather x1, waiting for transfers between devices: 0.01 us -> 4.87 us  [body(): lax.all_gather(after(grad_units, *dcq_pieces[1:]), 'ctx', axis=0)]
    reduce_scatter x2, waiting for transfers between devices: 9.6 us -> 14 us  [sum_z(): return lax.psum_scatter(value, 'fsdp', scatter_dimension=0, tiled=True)]
    unnamed x169 -> x167, local copies, waits for them, and re-layouts: 14.6 us -> 13.9 us
  transfers between devices with their start and end apart: 70 -> 70, of which waited for: 30 -> 28; matrix products, arithmetic and copies ran while one was open for 12% -> 12% of each run, Pallas kernels for 27% -> 27%
where the time goes in v1:
time: 417 us; the launch traced here: 409 us
  waiting for transfers between devices  151 us (36%)
  Pallas kernels  114 us (27%)
  starting transfers between devices  64.5 us (15%)
  local copies, waits for them, and re-layouts  33 us (8%)
  other arithmetic  17.6 us (4%)
  between operations  15.6 us (4%)
  matrix products  13.3 us (3%)
    ppermute x63, waiting for transfers between devices, send(): return lax.ppermute(value, axis, [(i, target(i)) for i in range(count)])  131 us
    pallas_call x15, Pallas kernels, run(): pl.pallas_call(kernel, in_specs=[smem] * len(scalars) + [vmem] * len(arra...  113 us
    ppermute x63, starting transfers between devices, send(): return lax.ppermute(value, axis, [(i, target(i)) for i in range(count)])  63.2 us
    reduce_scatter x2, waiting for transfers between devices, sum_z(): return lax.psum_scatter(value, 'fsdp', scatter_dimension=0, tiled=True)  14 us
    unnamed x167, local copies, waits for them, and re-layouts  13.9 us
    dot_general x12, matrix products, dot_tn(): lax.dot_general(a, b, (((0,), (0,)), ((), ())), preferred_element_type=F32)  13.3 us
  transfers between devices with their start and end apart: 70, of which 28 were waited for; matrix products, arithmetic and copies ran while one was open for 12% of the time, Pallas kernels for 27%

profile of v1, /device:TPU:0, one launch (start us, length us, event | category | flops | bytes accessed | tf_op | source)
XLA Modules:
  0.0 408.8 jit_solution(10822989891354225615)
XLA Ops:
  13.5 3.1 collective-permute-start
  16.5 2.6 collective-permute-start.4
  24.5 7.0 %collective-permute-done.refs_5_ = bf16[272,640]{1,0:T(8,128)(2,1)} collective-permute-done((bf16[272,640]{1,0:T(8,128)(2,1)S(1)}, bf16[272,640]{1,0:T(8,128)(2,1)}, u32[]{:S(2)}, u32[]{:S(2)}) %collective-permute-start) | collective-permute-done | bytes 348192 | tf_op jit(solution)/shard_map/ppermute | solution.py:47
  33.8 2.8 constant_dynamic-slice_fusion.11
  36.6 7.0 %collective-permute-done.4.refs_6_ = bf16[272,640]{1,0:T(8,128)(2,1)} collective-permute-done((bf16[272,640]{1,0:T(8,128)(2,1)S(1)}, bf16[272,640]{1,0:T(8,128)(2,1)}, u32[]{:S(2)}, u32[]{:S(2)}) %collective-permute-start.4) | collective-permute-done | bytes 348192 | tf_op jit(solution)/shard_map/ppermute | solution.py:47
  49.0 9.9 %collective-permute-done.2.refs_2_ = bf16[128,1024]{1,0:T(8,128)(2,1)S(1)} collective-permute-done((bf16[128,1024]{1,0:T(8,128)(2,1)}, bf16[128,1024]{1,0:T(8,128)(2,1)S(1)}, u32[]{:S(2)}, u32[]{:S(2)}) %collective-permute-start.2) | collective-permute-done | bytes 262176 | tf_op jit(solution)/shard_map/ppermute | solution.py:47
  59.8 6.7 %self_project.1 = (bf16[512,1024]{1,0:T(8,128)(2,1)}, bf16[512,1024]{1,0:T(8,128)(2,1)}, bf16[512,256]{1,0:T(8,128)(2,1)}, bf16[512,512]{1,0:T(8,128)(2,1)}, f32...) custom-call(s32[2]{0:T(128)} %pad_add_fusion.2.place, s32[4]{0:T(128)} %get-tuple-element.258.corder, ...), custom_call_target="tpu_custom_call" | custom-call | flops 1150000000 | bytes 1000000 | tf_op jit(solution)/shard_map/self_project/pallas_call | solution.py:324
  69.6 7.6 %collective-permute-start.10 = (bf16[256,384]{1,0:T(8,128)(2,1)S(1)}, bf16[256,384]{1,0:T(8,128)(2,1)S(1)}, u32[]{:S(2)}, u32[]{:S(2)}) collective-permute-start(bf16[256,384]{1,0:T(8,128)(2,1)S(1)} %copy-done.23), channel_id=1, source_target_pairs={{0,2},{1,3},{2,0},{3,1},{4,6},{5,7},{6,4},{7,5},{8,10},{9,11},{10,... | collective-permute-start | bytes 589832 | tf_op jit(solution)/shard_map/ppermute | solution.py:47
  80.0 6.0 %self_attend.1 = (bf16[1024,256]{1,0:T(8,128)(2,1)}, bf16[1024,256]{1,0:T(8,128)(2,1)}, bf16[512,256]{1,0:T(8,128)(2,1)}, f32[1,2048]{1,0:T(1,128)}) custom-call(s32[2]{0:T(128)} %pad_add_fusion.2.place, bf16[512,256]{1,0:T(8,128)(2,1)} %get-tuple-element.119.q_ref, bf16[512,512]{1,0:T(8,128)(2,1)} %get-tuple-element.121.mine_ref, ...), custom_call_target="tpu_custom_call" | custom-call | flops 1150000000 | bytes 1000000 | tf_op jit(solution)/shard_map/self_attend/pallas_call | solution.py:324
  86.0 5.4 %collective-permute-done.10 = bf16[256,384]{1,0:T(8,128)(2,1)S(1)} collective-permute-done((bf16[256,384]{1,0:T(8,128)(2,1)S(1)}, bf16[256,384]{1,0:T(8,128)(2,1)S(1)}, u32[]{:S(2)}, u32[]{:S(2)}) %collective-permute-start.10) | collective-permute-done | bytes 196640 | tf_op jit(solution)/shard_map/ppermute | solution.py:47
  100.2 8.9 %collective-permute-done.18.refs_5_.refs_9_ = bf16[4,256,256]{2,1,0:T(8,128)(2,1)S(1)} collective-permute-done((bf16[4,256,256]{2,1,0:T(8,128)(2,1)S(1)}, bf16[4,256,256]{2,1,0:T(8,128)(2,1)S(1)}, u32[]{:S(2)}, u32[]{:S(2)}) %collective-permute-start.18) | collective-permute-done | bytes 524320 | tf_op jit(solution)/shard_map/ppermute | solution.py:47
  109.1 2.6 collective-permute-start.20
  112.6 5.1 %encoder_block.1 = (bf16[1024,512]{1,0:T(8,128)(2,1)}, bf16[1024,512]{1,0:T(8,128)(2,1)}) custom-call(s32[2]{0:T(128)} %pad_add_fusion.2.place, s32[4]{0:T(128)} %get-tuple-element.259.zorder, bf16[8,256,1024]{2,1,0:T(8,128)(2,1)} %all-gather.10.cloned.1.call-done.enc_ref, bf16[4,256,384]{2,1,0:T(8,128)(2,1)} %copy-done.14, bf16[4,256,384]{2,1,0:T(8,128)(2,1)} %copy-done.22), custom_call_target="tpu_custom_call" | custom-call | flops 1150000000 | bytes 1000000 | tf_op jit(solution)/shard_map/encoder_block/pallas_call | solution.py:324
  122.6 6.2 %collective-permute-done.17.refs_3_ = bf16[512,256]{1,0:T(8,128)(2,1)} collective-permute-done((bf16[512,256]{1,0:T(8,128)(2,1)}, bf16[512,256]{1,0:T(8,128)(2,1)}, u32[]{:S(2)}, u32[]{:S(2)}) %collective-permute-start.17) | collective-permute-done | bytes 262176 | tf_op jit(solution)/shard_map/ppermute | solution.py:47
  132.8 2.0 collective-permute-start.26
  138.9 15.6 %cross_block.1 = (bf16[2048,256]{1,0:T(8,128)(2,1)}, bf16[2048,256]{1,0:T(8,128)(2,1)}, f32[512,1024]{1,0:T(8,128)}, bf16[512,1024]{1,0:T(8,128)(2,1)}, bf16[512...) custom-call(s32[2]{0:T(128)} %pad_add_fusion.2.place, ...), custom_call_target="tpu_custom_call" | custom-call | flops 6899999744 | bytes 6000000 | tf_op jit(solution)/shard_map/cross_block/pallas_call | solution.py:324
  158.4 5.2 %collective-permute-done.28.refs_5_ = bf16[512,256]{1,0:T(8,128)(2,1)S(1)} collective-permute-done((bf16[512,256]{1,0:T(8,128)(2,1)}, bf16[512,256]{1,0:T(8,128)(2,1)S(1)}, u32[]{:S(2)}, u32[]{:S(2)}) %collective-permute-start.28) | collective-permute-done | bytes 262176 | tf_op jit(solution)/shard_map/ppermute | solution.py:47
  163.6 2.4 collective-permute-done.29.refs_6_
  169.4 2.7 collective-permute-done.31.refs_17_
  173.5 14.0 %ffn_block.1 = (bf16[512,1024]{1,0:T(8,128)(2,1)}, bf16[512,1024]{1,0:T(8,128)(2,1)}, bf16[512,1024]{1,0:T(8,128)(2,1)}, bf16[512,384]{1,0:T(8,128)(2,1)}, bf16[...) custom-call(s32[2]{0:T(128)} %pad_add_fusion.2.place, ...), custom_call_target="tpu_custom_call" | custom-call | flops 16099999744 | bytes 14000000 | tf_op jit(solution)/shard_map/ffn_block/pallas_call | solution.py:324
  191.1 11.0 %collective-permute-done.32.refs_0_ = bf16[128,1024]{1,0:T(8,128)(2,1)S(1)} collective-permute-done((bf16[128,1024]{1,0:T(8,128)(2,1)}, bf16[128,1024]{1,0:T(8,128)(2,1)S(1)}, u32[]{:S(2)}, u32[]{:S(2)}) %collective-permute-start.32) | collective-permute-done | bytes 262176 | tf_op jit(solution)/shard_map/ppermute | solution.py:47
  202.7 5.1 %collective-permute-done.34.refs_2_ = bf16[128,1024]{1,0:T(8,128)(2,1)S(1)} collective-permute-done((bf16[128,1024]{1,0:T(8,128)(2,1)}, bf16[128,1024]{1,0:T(8,128)(2,1)S(1)}, u32[]{:S(2)}, u32[]{:S(2)}) %collective-permute-start.34) | collective-permute-done | bytes 262176 | tf_op jit(solution)/shard_map/ppermute | solution.py:47
  207.8 2.6 convolution_convert_fusion
  212.3 2.7 collective-permute-done.36
  218.1 2.8 norm_grad.2
  224.3 5.9 %collective-permute-done.37.refs_1_ = bf16[128,1024]{1,0:T(8,128)(2,1)S(1)} collective-permute-done((bf16[128,1024]{1,0:T(8,128)(2,1)}, bf16[128,1024]{1,0:T(8,128)(2,1)S(1)}, u32[]{:S(2)}, u32[]{:S(2)}) %collective-permute-start.37) | collective-permute-done | bytes 262176 | tf_op jit(solution)/shard_map/ppermute | solution.py:47
  230.2 5.9 %collective-permute-done.38.refs_2_ = bf16[128,1024]{1,0:T(8,128)(2,1)S(1)} collective-permute-done((bf16[128,1024]{1,0:T(8,128)(2,1)}, bf16[128,1024]{1,0:T(8,128)(2,1)S(1)}, u32[]{:S(2)}, u32[]{:S(2)}) %collective-permute-start.38) | collective-permute-done | bytes 262176 | tf_op jit(solution)/shard_map/ppermute | solution.py:47
  236.0 4.1 %ffn_output.1 = (f32[128,1024]{1,0:T(8,128)}, bf16[128,1024]{1,0:T(8,128)(2,1)}, bf16[128,1024]{1,0:T(8,128)(2,1)}, bf16[128,1024]{1,0:T(8,128)(2,1)}) custom-call(s32[2]{0:T(128)} %pad_add_fusion.2.place, bf16[512,384]{1,0:T(8,128)(2,1)} %get-tuple-element.152.act0_ref, bf16[512,384]{1,0:T(8,128)(2,1)} %get-tuple-element.147.act1_ref, ...), custom_call_target="tpu_custom_call" | custom-call | flops 4600000000 | bytes 4000000 | tf_op jit(solution)/shard_map/ffn_output/pallas_call | solution.py:324
  243.7 12.7 %cross_grad.1 = (bf16[512,1024]{1,0:T(8,128)(2,1)}, bf16[512,256]{1,0:T(8,128)(2,1)}, f32[1024,512]{1,0:T(8,128)}, bf16[1024,512]{1,0:T(8,128)(2,1)}) custom-call(s32[2]{0:T(128)} %pad_add_fusion.2.place, s32[4]{0:T(128)} %get-tuple-element.258.corder, s32[1]{0:T(128)} %bitcast.19.count_ref, s32[8]{0:T(128)} %copy-done.78, s32[8]{0:T(128)} %copy-done.79, ...), custom_call_target="tpu_custom_call" | custom-call | flops 14949999616 | bytes 13000000 | tf_op jit(solution)/shard_map/cross_grad/pallas_call | solution.py:324
  256.5 2.0 add_convert_fusion.2
  262.0 6.0 %collective-permute-done.43.refs_1_ = bf16[512,256]{1,0:T(8,128)(2,1)S(1)} collective-permute-done((bf16[512,256]{1,0:T(8,128)(2,1)}, bf16[512,256]{1,0:T(8,128)(2,1)S(1)}, u32[]{:S(2)}, u32[]{:S(2)}) %collective-permute-start.43) | collective-permute-done | bytes 262176 | tf_op jit(solution)/shard_map/ppermute | solution.py:47
  268.0 4.3 %collective-permute-done.44.refs_2_ = bf16[512,256]{1,0:T(8,128)(2,1)S(1)} collective-permute-done((bf16[512,256]{1,0:T(8,128)(2,1)}, bf16[512,256]{1,0:T(8,128)(2,1)S(1)}, u32[]{:S(2)}, u32[]{:S(2)}) %collective-permute-start.44) | collective-permute-done | bytes 262176 | tf_op jit(solution)/shard_map/ppermute | solution.py:47
  275.9 7.1 %encoder_grad.1 = (bf16[1024,512]{1,0:T(8,128)(2,1)}, f32[256,1024]{1,0:T(8,128)}, bf16[256,1024]{1,0:T(8,128)(2,1)}, bf16[256,1024]{1,0:T(8,128)(2,1)}, bf16[256,1024]{1,0:T(8,128)(2,1)}) custom-call(s32[2]{0:T(128)} %pad_add_fusion.2.place, f32[1024,512]{1,0:T(8,128)} %get-tuple-element.166.keep_ref, bf16[1024,512]{1,0:T(8,128)(2,1)} %collective-permute-done.46.come_ref, ...), custom_call_target="tpu_custom_call" | custom-call | flops 8049999872 | bytes 7000000 | tf_op jit(solution)/shard_map/encoder_grad/pallas_call | solution.py:324
  283.0 2.0 constant_dynamic-slice_fusion.8
  288.2 2.5 fusion.3
  290.6 14.7 %self_grad.1 = (bf16[512,1024]{1,0:T(8,128)(2,1)}, bf16[512,256]{1,0:T(8,128)(2,1)}, f32[512,512]{1,0:T(8,128)}, bf16[512,512]{1,0:T(8,128)(2,1)}, f32[4,32,128]...) custom-call(s32[2]{0:T(128)} %pad_add_fusion.2.place, s32[8]{0:T(128)} %stack.105.order, ...), custom_call_target="tpu_custom_call" | custom-call | flops 17250000896 | bytes 15000000 | tf_op jit(solution)/shard_map/self_grad/pallas_call | solution.py:324
  305.9 4.9 %all-gather.16.cloned.1.call-done = bf16[3008,768]{1,0:T(8,128)(2,1)} async-done(((bf16[376,768]{1,0:T(8,128)(2,1)}), bf16[3008,768]{1,0:T(8,128)(2,1)}) %all-gather.16.cloned.1.call-update) | async-done | bytes 4620304 | tf_op jit(solution)/shard_map/all_gather | solution.py:997
  312.9 5.5 %self_close.1 = (bf16[512,768]{1,0:T(8,128)(2,1)}, f32[1,1024]{1,0:T(1,128)}, f32[128,1024]{1,0:T(8,128)}, bf16[384,1024]{1,0:T(8,128)(2,1)}, bf16[384,1024]{1,0:T(8,128)(2,1)}, /*index=5*/bf16[384,1024]{1,0:T(8,128)(2,1)}) custom-call(s32[2]{0:T(128)} %pad_add_fusion.2.place, bf16[512,1024]{1,0:T(8,128)(2,1)} %get-tuple-element.117.x_ref, ...), custom_call_target="tpu_custom_call" | custom-call | flops 4600000000 | bytes 4000000 | tf_op jit(solution)/shard_map/self_close/pallas_call | solution.py:324
  326.8 14.0 %reduce-scatter.5.cloned.1.call-done = bf16[256,512]{1,0:T(8,128)(2,1)} async-done(((bf16[1024,512]{1,0:T(8,128)(2,1)}), bf16[256,512]{1,0:T(8,128)(2,1)}) %reduce-scatter.5.cloned.1.call-update) | async-done | bytes 262160 | tf_op jit(solution)/shard_map/reduce_scatter | solution.py:930
  345.4 12.4 %collective-permute-done.53 = bf16[272,512]{1,0:T(8,128)(2,1)S(1)} collective-permute-done((bf16[272,512]{1,0:T(8,128)(2,1)S(1)}, bf16[272,512]{1,0:T(8,128)(2,1)S(1)}, u32[]{:S(2)}, u32[]{:S(2)}) %collective-permute-start.53) | collective-permute-done | bytes 278560 | tf_op jit(solution)/shard_map/ppermute | solution.py:47
  358.1 5.7 %collective-permute-done.51.refs_2_ = bf16[384,1024]{1,0:T(8,128)(2,1)} collective-permute-done((bf16[384,1024]{1,0:T(8,128)(2,1)}, bf16[384,1024]{1,0:T(8,128)(2,1)}, u32[]{:S(2)}, u32[]{:S(2)}) %collective-permute-start.51) | collective-permute-done | bytes 786464 | tf_op jit(solution)/shard_map/ppermute | solution.py:47
  363.7 3.2 norm_grad.3
  367.0 7.4 %spread_units.1 = (f32[256,5632]{1,0:T(8,128)}, f32[704,1024]{1,0:T(8,128)}) custom-call(bf16[8,376,768]{2,1,0:T(8,128)(2,1)} %bitcast.116), custom_call_target="tpu_custom_call" | custom-call | flops 6899999744 | bytes 6000000 | tf_op jit(solution)/shard_map/spread_units/pallas_call | solution.py:324
  376.8 6.3 %collective-permute-done.56.refs_1_ = bf16[272,512]{1,0:T(8,128)(2,1)S(1)} collective-permute-done((bf16[272,512]{1,0:T(8,128)(2,1)S(1)}, bf16[272,512]{1,0:T(8,128)(2,1)S(1)}, u32[]{:S(2)}, u32[]{:S(2)}) %collective-permute-start.56) | collective-permute-done | bytes 278560 | tf_op jit(solution)/shard_map/ppermute | solution.py:47
  385.5 4.2 %collective-permute-done.58.refs_3_ = bf16[272,512]{1,0:T(8,128)(2,1)S(1)} collective-permute-done((bf16[272,512]{1,0:T(8,128)(2,1)S(1)}, bf16[272,512]{1,0:T(8,128)(2,1)S(1)}, u32[]{:S(2)}, u32[]{:S(2)}) %collective-permute-start.58) | collective-permute-done | bytes 278560 | tf_op jit(solution)/shard_map/ppermute | solution.py:47
  389.6 2.8 add_bitcast_fusion
  394.0 3.8 spread.1
  397.8 3.9 spread_stacked.1
  (373 shorter events, 105.3 us)
Async XLA Ops:
  7.2 104.5 %all-gather.10.cloned.1.call-start = ((), (), s32[]{:S(2)}) async-start(), calls=%async_computation.2 | async-start | bytes 4718592 | tf_op jit(solution)/shard_map/all_gather | solution.py:803
  7.9 150.5 %all-gather.12.cloned.1.call-start = ((), (), s32[]{:S(2)}) async-start(), calls=%async_computation.5 | async-start | bytes 2887680 | tf_op jit(solution)/shard_map/all_gather | solution.py:890
  13.5 18.0 %collective-permute-start = (bf16[272,640]{1,0:T(8,128)(2,1)S(1)}, bf16[272,640]{1,0:T(8,128)(2,1)}, u32[]{:S(2)}, u32[]{:S(2)}) collective-permute-start(bf16[272,640]{1,0:T(8,128)(2,1)S(1)} %first_weights.2.refs_4_), channel_id=1, source_target_pairs={{0,1},{1,0},{2,3},{3,2},{4,5},{5,4},{6,7},{7,6},{8,9},{9,8},{10,11... | collective-permute-start | bytes 1044488 | tf_op jit(solution)/shard_map/ppermute | solution.py:47
  16.5 27.0 %collective-permute-start.4 = (bf16[272,640]{1,0:T(8,128)(2,1)S(1)}, bf16[272,640]{1,0:T(8,128)(2,1)}, u32[]{:S(2)}, u32[]{:S(2)}) collective-permute-start(bf16[272,640]{1,0:T(8,128)(2,1)S(1)} %first_weights.2.refs_4_), channel_id=1, source_target_pairs={{0,2},{1,3},{2,0},{3,1},{4,6},{5,7},{6,4},{7,5},{8,10},{9,11},{10,... | collective-permute-start | bytes 1044488 | tf_op jit(solution)/shard_map/ppermute | solution.py:47
  19.1 24.4 %collective-permute-start.5 = (bf16[272,640]{1,0:T(8,128)(2,1)S(1)}, bf16[272,640]{1,0:T(8,128)(2,1)}, u32[]{:S(2)}, u32[]{:S(2)}) collective-permute-start(bf16[272,640]{1,0:T(8,128)(2,1)S(1)} %first_weights.2.refs_4_), channel_id=1, source_target_pairs={{0,3},{1,2},{2,1},{3,0},{4,7},{5,6},{6,5},{7,4},{8,11},{9,10},{10,... | collective-permute-start | bytes 1044488 | tf_op jit(solution)/shard_map/ppermute | solution.py:47
  31.5 14.7 %collective-permute-start.1 = (bf16[128,1024]{1,0:T(8,128)(2,1)}, bf16[128,1024]{1,0:T(8,128)(2,1)}, u32[]{:S(2)}, u32[]{:S(2)}) collective-permute-start(bf16[128,1024]{1,0:T(8,128)(2,1)} %bitcast.126), channel_id=1, source_target_pairs={{0,8},{4,12},{8,0},{12,4},{16,24},{20,28},{24,16},{28,20},{1,9},{5... | collective-permute-start | bytes 786440 | tf_op jit(solution)/shard_map/ppermute | solution.py:47
  36.6 22.3 %collective-permute-start.6 = (bf16[272,640]{1,0:T(8,128)(2,1)}, bf16[272,640]{1,0:T(8,128)(2,1)S(1)}, u32[]{:S(2)}, u32[]{:S(2)}) collective-permute-start(bf16[272,640]{1,0:T(8,128)(2,1)} %collective-permute-done.refs_5_), channel_id=1, source_target_pairs={{0,4},{4,0},{8,12},{12,8},{16,20},{20,16},{24,28},{28,24},{1,5},{5... | collective-permute-start | bytes 1044488 | tf_op jit(solution)/shard_map/ppermute | solution.py:47
  43.5 15.4 %collective-permute-start.7 = (bf16[272,640]{1,0:T(8,128)(2,1)}, bf16[272,640]{1,0:T(8,128)(2,1)}, u32[]{:S(2)}, u32[]{:S(2)}) collective-permute-start(bf16[272,640]{1,0:T(8,128)(2,1)} %collective-permute-done.4.refs_6_), channel_id=1, source_target_pairs={{0,4},{4,0},{8,12},{12,8},{16,20},{20,16},{24,28},{28,24},{1,5},{5... | collective-permute-start | bytes 1044488 | tf_op jit(solution)/shard_map/ppermute | solution.py:47
  43.6 15.4 %collective-permute-start.8 = (bf16[272,640]{1,0:T(8,128)(2,1)}, bf16[272,640]{1,0:T(8,128)(2,1)}, u32[]{:S(2)}, u32[]{:S(2)}) collective-permute-start(bf16[272,640]{1,0:T(8,128)(2,1)} %collective-permute-done.5.refs_7_), channel_id=1, source_target_pairs={{0,4},{4,0},{8,12},{12,8},{16,20},{20,16},{24,28},{28,24},{1,5},{5... | collective-permute-start | bytes 1044488 | tf_op jit(solution)/shard_map/ppermute | solution.py:47
  44.7 14.2 %collective-permute-start.2 = (bf16[128,1024]{1,0:T(8,128)(2,1)}, bf16[128,1024]{1,0:T(8,128)(2,1)S(1)}, u32[]{:S(2)}, u32[]{:S(2)}) collective-permute-start(bf16[128,1024]{1,0:T(8,128)(2,1)} %bitcast.127), channel_id=1, source_target_pairs={{0,16},{4,20},{8,24},{12,28},{16,0},{20,4},{24,8},{28,12},{1,17},{... | collective-permute-start | bytes 786440 | tf_op jit(solution)/shard_map/ppermute | solution.py:47
  46.2 12.6 %collective-permute-start.3 = (bf16[128,1024]{1,0:T(8,128)(2,1)}, bf16[128,1024]{1,0:T(8,128)(2,1)S(1)}, u32[]{:S(2)}, u32[]{:S(2)}) collective-permute-start(bf16[128,1024]{1,0:T(8,128)(2,1)} %bitcast.128), channel_id=1, source_target_pairs={{0,24},{4,28},{8,16},{12,20},{16,8},{20,12},{24,0},{28,4},{1,25},{... | collective-permute-start | bytes 786440 | tf_op jit(solution)/shard_map/ppermute | solution.py:47
  66.6 12.6 %collective-permute-start.12 = (bf16[512,512]{1,0:T(8,128)(2,1)}, bf16[512,512]{1,0:T(8,128)(2,1)S(1)}, u32[]{:S(2)}, u32[]{:S(2)}) collective-permute-start(bf16[512,512]{1,0:T(8,128)(2,1)} %get-tuple-element.121.mine_ref), channel_id=1, source_target_pairs={{0,4},{4,0},{8,12},{12,8},{16,20},{20,16},{24,28},{28,24},{1,5},{5... | collective-permute-start | bytes 1572872 | tf_op jit(solution)/shard_map/ppermute | solution.py:47
  69.6 21.8 %collective-permute-start.10 = (bf16[256,384]{1,0:T(8,128)(2,1)S(1)}, bf16[256,384]{1,0:T(8,128)(2,1)S(1)}, u32[]{:S(2)}, u32[]{:S(2)}) collective-permute-start(bf16[256,384]{1,0:T(8,128)(2,1)S(1)} %copy-done.23), channel_id=1, source_target_pairs={{0,2},{1,3},{2,0},{3,1},{4,6},{5,7},{6,4},{7,5},{8,10},{9,11},{10,... | collective-permute-start | bytes 589832 | tf_op jit(solution)/shard_map/ppermute | solution.py:47
  77.2 14.2 %collective-permute-start.11 = (bf16[256,384]{1,0:T(8,128)(2,1)S(1)}, bf16[256,384]{1,0:T(8,128)(2,1)S(1)}, u32[]{:S(2)}, u32[]{:S(2)}) collective-permute-start(bf16[256,384]{1,0:T(8,128)(2,1)S(1)} %copy-done.23), channel_id=1, source_target_pairs={{0,3},{1,2},{2,1},{3,0},{4,7},{5,6},{6,5},{7,4},{8,11},{9,10},{10,... | collective-permute-start | bytes 589832 | tf_op jit(solution)/shard_map/ppermute | solution.py:47
  78.5 14.0 %collective-permute-start.9 = (bf16[256,384]{1,0:T(8,128)(2,1)S(1)}, bf16[256,384]{1,0:T(8,128)(2,1)S(1)}, u32[]{:S(2)}, u32[]{:S(2)}) collective-permute-start(bf16[256,384]{1,0:T(8,128)(2,1)S(1)} %copy-done.23), channel_id=1, source_target_pairs={{0,1},{1,0},{2,3},{3,2},{4,5},{5,4},{6,7},{7,6},{8,9},{9,8},{10,11... | collective-permute-start | bytes 589832 | tf_op jit(solution)/shard_map/ppermute | solution.py:47
  92.7 125.3 %all-gather.14.cloned.1.call-start = ((), (), s32[]{:S(2)}) async-start(), calls=%async_computation.6 | async-start | bytes 2359296 | tf_op jit(solution)/shard_map/all_gather | solution.py:911
  95.0 16.7 %collective-permute-start.13 = (bf16[4,256,384]{2,1,0:T(8,128)(2,1)S(1)}, bf16[4,256,384]{2,1,0:T(8,128)(2,1)S(1)}, u32[]{:S(2)}, u32[]{:S(2)}) collective-permute-start(bf16[4,256,384]{2,1,0:T(8,128)(2,1)S(1)} %pad_maximum_fusion.2.refs_0_.refs_12_), channel_id=1, source_target_pairs={{0,4},{4,0},{8,12},{12,8},{16,20},{20,16},{24,28},{28,24},{1,5},{5... | collective-permute-start | bytes 2359304 | tf_op jit(solution)/shard_map/ppermute | solution.py:47
  96.1 13.0 %collective-permute-start.18 = (bf16[4,256,256]{2,1,0:T(8,128)(2,1)S(1)}, bf16[4,256,256]{2,1,0:T(8,128)(2,1)S(1)}, u32[]{:S(2)}, u32[]{:S(2)}) collective-permute-start(bf16[4,256,256]{2,1,0:T(8,128)(2,1)S(1)} %pad_maximum_fusion.3.refs_4_.refs_8_), channel_id=1, source_target_pairs={{0,8},{4,20},{8,0},{12,28},{16,24},{20,4},{24,16},{28,12},{1,9},{5... | collective-permute-start | bytes 1572872 | tf_op jit(solution)/shard_map/ppermute | solution.py:47
  98.6 19.7 %collective-permute-start.19 = (bf16[4,256,256]{2,1,0:T(8,128)(2,1)S(1)}, bf16[4,256,256]{2,1,0:T(8,128)(2,1)S(1)}, u32[]{:S(2)}, u32[]{:S(2)}) collective-permute-start(bf16[4,256,256]{2,1,0:T(8,128)(2,1)S(1)} %pad_maximum_fusion.3.refs_4_.refs_8_), channel_id=1, source_target_pairs={{0,16},{4,12},{8,24},{12,4},{16,0},{20,28},{24,8},{28,20},{1,17},{... | collective-permute-start | bytes 1572872 | tf_op jit(solution)/shard_map/ppermute | solution.py:47
  100.2 20.4 %collective-permute-start.21 = (bf16[4,256,256]{2,1,0:T(8,128)(2,1)S(1)}, bf16[4,256,256]{2,1,0:T(8,128)(2,1)}, u32[]{:S(2)}, u32[]{:S(2)}) collective-permute-start(bf16[4,256,256]{2,1,0:T(8,128)(2,1)S(1)} %pad_maximum_fusion.3.refs_4_.refs_8_), channel_id=1, source_target_pairs={{0,4},{4,0},{8,12},{12,8},{16,20},{20,16},{24,28},{28,24},{1,5},{5... | collective-permute-start | bytes 1572872 | tf_op jit(solution)/shard_map/ppermute | solution.py:47
  109.1 11.6 %collective-permute-start.20 = (bf16[4,256,256]{2,1,0:T(8,128)(2,1)S(1)}, bf16[4,256,256]{2,1,0:T(8,128)(2,1)}, u32[]{:S(2)}, u32[]{:S(2)}) collective-permute-start(bf16[4,256,256]{2,1,0:T(8,128)(2,1)S(1)} %collective-permute-done.18.refs_5_.refs_9_), channel_id=1, source_target_pairs={{0,16},{4,12},{8,24},{12,4},{16,0},{20,28},{24,8},{28,20},{1,17},{... | collective-permute-start | bytes 1572872 | tf_op jit(solution)/shard_map/ppermute | solution.py:47
  117.7 19.5 %collective-permute-start.14 = (bf16[1024,512]{1,0:T(8,128)(2,1)}, bf16[1024,512]{1,0:T(8,128)(2,1)S(1)}, u32[]{:S(2)}, u32[]{:S(2)}) collective-permute-start(bf16[1024,512]{1,0:T(8,128)(2,1)} %get-tuple-element.128.kvm_ref), channel_id=1, source_target_pairs={{0,4},{4,0},{8,12},{12,8},{16,20},{20,16},{24,28},{28,24},{1,5},{5... | collective-permute-start | bytes 3145736 | tf_op jit(solution)/shard_map/ppermute | solution.py:47
  120.7 16.5 %collective-permute-start.24 = (bf16[4,256,256]{2,1,0:T(8,128)(2,1)}, bf16[4,256,256]{2,1,0:T(8,128)(2,1)S(1)}, u32[]{:S(2)}, u32[]{:S(2)}) collective-permute-start(bf16[4,256,256]{2,1,0:T(8,128)(2,1)} %collective-permute-done.20.refs_7_.refs_11_), channel_id=1, source_target_pairs={{0,4},{4,0},{8,12},{12,8},{16,20},{20,16},{24,28},{28,24},{1,5},{5... | collective-permute-start | bytes 1572872 | tf_op jit(solution)/shard_map/ppermute | solution.py:47
  121.2 11.6 %collective-permute-start.15 = (bf16[512,256]{1,0:T(8,128)(2,1)}, bf16[512,256]{1,0:T(8,128)(2,1)S(1)}, u32[]{:S(2)}, u32[]{:S(2)}) collective-permute-start(bf16[512,256]{1,0:T(8,128)(2,1)} %get-tuple-element.123.refs_0_), channel_id=1, source_target_pairs={{0,8},{4,12},{8,0},{12,4},{16,24},{20,28},{24,16},{28,20},{1,9},{5... | collective-permute-start | bytes 786440 | tf_op jit(solution)/shard_map/ppermute | solution.py:47
  129.4 25.1 %collective-permute-start.25 = (bf16[128,1024]{1,0:T(8,128)(2,1)}, bf16[128,1024]{1,0:T(8,128)(2,1)}, u32[]{:S(2)}, u32[]{:S(2)}) collective-permute-start(bf16[128,1024]{1,0:T(8,128)(2,1)} %bitcast.121), channel_id=1, source_target_pairs={{0,8},{4,12},{8,0},{12,4},{16,24},{20,28},{24,16},{28,20},{1,9},{5... | collective-permute-start | bytes 786440 | tf_op jit(solution)/shard_map/ppermute | solution.py:47
  132.8 21.7 %collective-permute-start.26 = (bf16[128,1024]{1,0:T(8,128)(2,1)}, bf16[128,1024]{1,0:T(8,128)(2,1)}, u32[]{:S(2)}, u32[]{:S(2)}) collective-permute-start(bf16[128,1024]{1,0:T(8,128)(2,1)} %bitcast.122), channel_id=1, source_target_pairs={{0,16},{4,20},{8,24},{12,28},{16,0},{20,4},{24,8},{28,12},{1,17},{... | collective-permute-start | bytes 786440 | tf_op jit(solution)/shard_map/ppermute | solution.py:47
  136.2 18.3 %collective-permute-start.27 = (bf16[128,1024]{1,0:T(8,128)(2,1)}, bf16[128,1024]{1,0:T(8,128)(2,1)}, u32[]{:S(2)}, u32[]{:S(2)}) collective-permute-start(bf16[128,1024]{1,0:T(8,128)(2,1)} %bitcast.123), channel_id=1, source_target_pairs={{0,24},{4,28},{8,16},{12,20},{16,8},{20,12},{24,0},{28,4},{1,25},{... | collective-permute-start | bytes 786440 | tf_op jit(solution)/shard_map/ppermute | solution.py:47
  169.2 103.2 %reduce-scatter.3.cloned.1.call-start = ((), (), s32[]{:S(2)}) async-start(), calls=%async_computation.3 | async-start | bytes 2887680 | tf_op jit(solution)/shard_map/reduce_scatter | solution.py:930
  187.5 14.5 %collective-permute-start.32 = (bf16[128,1024]{1,0:T(8,128)(2,1)}, bf16[128,1024]{1,0:T(8,128)(2,1)S(1)}, u32[]{:S(2)}, u32[]{:S(2)}) collective-permute-start(bf16[128,1024]{1,0:T(8,128)(2,1)} %get-tuple-element.138), channel_id=1, source_target_pairs={{0,8},{4,12},{8,0},{12,4},{16,24},{20,28},{24,16},{28,20},{1,9},{5... | collective-permute-start | bytes 786440 | tf_op jit(solution)/shard_map/ppermute | solution.py:47
  188.3 14.4 %collective-permute-start.33 = (bf16[128,1024]{1,0:T(8,128)(2,1)}, bf16[128,1024]{1,0:T(8,128)(2,1)S(1)}, u32[]{:S(2)}, u32[]{:S(2)}) collective-permute-start(bf16[128,1024]{1,0:T(8,128)(2,1)} %get-tuple-element.139), channel_id=1, source_target_pairs={{0,16},{4,20},{8,24},{12,28},{16,0},{20,4},{24,8},{28,12},{1,17},{... | collective-permute-start | bytes 786440 | tf_op jit(solution)/shard_map/ppermute | solution.py:47
  190.3 17.5 %collective-permute-start.34 = (bf16[128,1024]{1,0:T(8,128)(2,1)}, bf16[128,1024]{1,0:T(8,128)(2,1)S(1)}, u32[]{:S(2)}, u32[]{:S(2)}) collective-permute-start(bf16[128,1024]{1,0:T(8,128)(2,1)} %get-tuple-element.140), channel_id=1, source_target_pairs={{0,24},{4,28},{8,16},{12,20},{16,8},{20,12},{24,0},{28,4},{1,25},{... | collective-permute-start | bytes 786440 | tf_op jit(solution)/shard_map/ppermute | solution.py:47
  218.0 92.7 %all-gather.16.cloned.1.call-start = ((), (), s32[]{:S(2)}) async-start(), calls=%async_computation.7 | async-start | bytes 5197824 | tf_op jit(solution)/shard_map/all_gather | solution.py:997
  222.1 13.9 %collective-permute-start.38 = (bf16[128,1024]{1,0:T(8,128)(2,1)}, bf16[128,1024]{1,0:T(8,128)(2,1)S(1)}, u32[]{:S(2)}, u32[]{:S(2)}) collective-permute-start(bf16[128,1024]{1,0:T(8,128)(2,1)} %get-tuple-element.151.refs_0_), channel_id=1, source_target_pairs={{0,16},{4,20},{8,24},{12,28},{16,0},{20,4},{24,8},{28,12},{1,17},{... | collective-permute-start | bytes 786440 | tf_op jit(solution)/shard_map/ppermute | solution.py:47
  222.8 13.3 %collective-permute-start.39 = (bf16[128,1024]{1,0:T(8,128)(2,1)}, bf16[128,1024]{1,0:T(8,128)(2,1)S(1)}, u32[]{:S(2)}, u32[]{:S(2)}) collective-permute-start(bf16[128,1024]{1,0:T(8,128)(2,1)} %get-tuple-element.151.refs_0_), channel_id=1, source_target_pairs={{0,24},{4,28},{8,16},{12,20},{16,8},{20,12},{24,0},{28,4},{1,25},{... | collective-permute-start | bytes 786440 | tf_op jit(solution)/shard_map/ppermute | solution.py:47
  240.2 16.3 %collective-permute-start.40 = (bf16[128,1024]{1,0:T(8,128)(2,1)}, bf16[128,1024]{1,0:T(8,128)(2,1)S(1)}, u32[]{:S(2)}, u32[]{:S(2)}) collective-permute-start(bf16[128,1024]{1,0:T(8,128)(2,1)} %get-tuple-element.156), channel_id=1, source_target_pairs={{0,8},{4,12},{8,0},{12,4},{16,24},{20,28},{24,16},{28,20},{1,9},{5... | collective-permute-start | bytes 786440 | tf_op jit(solution)/shard_map/ppermute | solution.py:47
  241.0 15.5 %collective-permute-start.41 = (bf16[128,1024]{1,0:T(8,128)(2,1)}, bf16[128,1024]{1,0:T(8,128)(2,1)S(1)}, u32[]{:S(2)}, u32[]{:S(2)}) collective-permute-start(bf16[128,1024]{1,0:T(8,128)(2,1)} %get-tuple-element.157), channel_id=1, source_target_pairs={{0,16},{4,20},{8,24},{12,28},{16,0},{20,4},{24,8},{28,12},{1,17},{... | collective-permute-start | bytes 786440 | tf_op jit(solution)/shard_map/ppermute | solution.py:47
  241.9 14.6 %collective-permute-start.42 = (bf16[128,1024]{1,0:T(8,128)(2,1)}, bf16[128,1024]{1,0:T(8,128)(2,1)}, u32[]{:S(2)}, u32[]{:S(2)}) collective-permute-start(bf16[128,1024]{1,0:T(8,128)(2,1)} %get-tuple-element.158), channel_id=1, source_target_pairs={{0,24},{4,28},{8,16},{12,20},{16,8},{20,12},{24,0},{28,4},{1,25},{... | collective-permute-start | bytes 786440 | tf_op jit(solution)/shard_map/ppermute | solution.py:47
  259.2 13.1 %collective-permute-start.44 = (bf16[512,256]{1,0:T(8,128)(2,1)}, bf16[512,256]{1,0:T(8,128)(2,1)S(1)}, u32[]{:S(2)}, u32[]{:S(2)}) collective-permute-start(bf16[512,256]{1,0:T(8,128)(2,1)} %get-tuple-element.168.refs_0_), channel_id=1, source_target_pairs={{0,16},{4,20},{8,24},{12,28},{16,0},{20,4},{24,8},{28,12},{1,17},{... | collective-permute-start | bytes 786440 | tf_op jit(solution)/shard_map/ppermute | solution.py:47
  260.1 12.2 %collective-permute-start.45 = (bf16[512,256]{1,0:T(8,128)(2,1)}, bf16[512,256]{1,0:T(8,128)(2,1)}, u32[]{:S(2)}, u32[]{:S(2)}) collective-permute-start(bf16[512,256]{1,0:T(8,128)(2,1)} %get-tuple-element.168.refs_0_), channel_id=1, source_target_pairs={{0,24},{4,28},{8,16},{12,20},{16,8},{20,12},{24,0},{28,4},{1,25},{... | collective-permute-start | bytes 786440 | tf_op jit(solution)/shard_map/ppermute | solution.py:47
  272.4 68.4 %reduce-scatter.5.cloned.1.call-start = ((), (), s32[]{:S(2)}) async-start(), calls=%async_computation.4 | async-start | bytes 1310720 | tf_op jit(solution)/shard_map/reduce_scatter | solution.py:930
  310.8 87.1 %all-gather.18.cloned.1.call-start = ((), (), s32[]{:S(2)}) async-start(), calls=%async_computation.8 | async-start | bytes 2359296 | tf_op jit(solution)/shard_map/all_gather | solution.py:1026
  321.4 20.0 %collective-permute-start.52 = (bf16[1024,512]{0,1:T(8,128)(2,1)}, bf16[1024,512]{0,1:T(8,128)(2,1)}, u32[]{:S(2)}, u32[]{:S(2)}) collective-permute-start(bf16[1024,512]{0,1:T(8,128)(2,1)} %pad_maximum_fusion.1), channel_id=1, source_target_pairs={{0,4},{4,0},{8,12},{12,8},{16,20},{20,16},{24,28},{28,24},{1,5},{5... | collective-permute-start | bytes 3145736 | tf_op jit(solution)/shard_map/ppermute | solution.py:47
  323.2 34.9 %collective-permute-start.49 = (bf16[384,1024]{1,0:T(8,128)(2,1)}, bf16[384,1024]{1,0:T(8,128)(2,1)}, u32[]{:S(2)}, u32[]{:S(2)}) collective-permute-start(bf16[384,1024]{1,0:T(8,128)(2,1)} %get-tuple-element.192), channel_id=1, source_target_pairs={{0,8},{4,12},{8,0},{12,4},{16,24},{20,28},{24,16},{28,20},{1,9},{5... | collective-permute-start | bytes 2359304 | tf_op jit(solution)/shard_map/ppermute | solution.py:47
  324.7 33.4 %collective-permute-start.50 = (bf16[384,1024]{1,0:T(8,128)(2,1)}, bf16[384,1024]{1,0:T(8,128)(2,1)}, u32[]{:S(2)}, u32[]{:S(2)}) collective-permute-start(bf16[384,1024]{1,0:T(8,128)(2,1)} %get-tuple-element.193), channel_id=1, source_target_pairs={{0,16},{4,20},{8,24},{12,28},{16,0},{20,4},{24,8},{28,12},{1,17},{... | collective-permute-start | bytes 2359304 | tf_op jit(solution)/shard_map/ppermute | solution.py:47
  325.3 38.5 %collective-permute-start.51 = (bf16[384,1024]{1,0:T(8,128)(2,1)}, bf16[384,1024]{1,0:T(8,128)(2,1)}, u32[]{:S(2)}, u32[]{:S(2)}) collective-permute-start(bf16[384,1024]{1,0:T(8,128)(2,1)} %get-tuple-element.194), channel_id=1, source_target_pairs={{0,24},{4,28},{8,16},{12,20},{16,8},{20,12},{24,0},{28,4},{1,25},{... | collective-permute-start | bytes 2359304 | tf_op jit(solution)/shard_map/ppermute | solution.py:47
  343.7 14.0 %collective-permute-start.53 = (bf16[272,512]{1,0:T(8,128)(2,1)S(1)}, bf16[272,512]{1,0:T(8,128)(2,1)S(1)}, u32[]{:S(2)}, u32[]{:S(2)}) collective-permute-start(bf16[272,512]{1,0:T(8,128)(2,1)S(1)} %get-tuple-element.237), channel_id=1, source_target_pairs={{0,1},{1,0},{2,3},{3,2},{4,5},{5,4},{6,7},{7,6},{8,9},{9,8},{10,11... | collective-permute-start | bytes 835592 | tf_op jit(solution)/shard_map/ppermute | solution.py:47
  343.8 30.5 %collective-permute-start.54 = (bf16[272,512]{1,0:T(8,128)(2,1)S(1)}, bf16[272,512]{1,0:T(8,128)(2,1)S(1)}, u32[]{:S(2)}, u32[]{:S(2)}) collective-permute-start(bf16[272,512]{1,0:T(8,128)(2,1)S(1)} %get-tuple-element.236), channel_id=1, source_target_pairs={{0,2},{1,3},{2,0},{3,1},{4,6},{5,7},{6,4},{7,5},{8,10},{9,11},{10,... | collective-permute-start | bytes 835592 | tf_op jit(solution)/shard_map/ppermute | solution.py:47
  357.8 16.6 %collective-permute-start.55 = (bf16[272,512]{1,0:T(8,128)(2,1)S(1)}, bf16[272,512]{1,0:T(8,128)(2,1)S(1)}, u32[]{:S(2)}, u32[]{:S(2)}) collective-permute-start(bf16[272,512]{1,0:T(8,128)(2,1)S(1)} %get-tuple-element.235), channel_id=1, source_target_pairs={{0,3},{1,2},{2,1},{3,0},{4,7},{5,6},{6,5},{7,4},{8,11},{9,10},{10,... | collective-permute-start | bytes 835592 | tf_op jit(solution)/shard_map/ppermute | solution.py:47
  (105 other events, 962.7 us)
Sparse Core Ops, SparseCore 0:
  9.9 43.3 all-gather.9
  92.8 50.8 all-gather.11
  169.3 34.6 all-gather.13
  218.1 46.3 reduce-scatter.2
  272.5 38.2 all-gather.15
  313.6 27.1 reduce-scatter.4
  342.6 36.3 all-gather.17
